TPU v7x, 512 devices: a whole 4x8x8 slice. The times are simulated.
512 devices in a mesh: lon: 64 (over y_lo, z, core), lat: 8 (over y_hi, x).
Axes of the slice: x: 4, y: 8 (y_hi: 2, y_lo: 4; y = y_hi * 4 + y_lo), z: 8, core: 2. Of those that a mesh axis runs over, the one named last changes fastest.
Arguments:
- final_adjoint: float32 [2, 38, 64, 8192], P(None, None, 'lat', 'lon'), may hold values from -6 to 6
- store: bfloat16 [4, 38, 16, 8, 8192], P(None, None, None, 'lat', 'lon'), may hold values from -6 to 6
- holder_offset: int32 [2, 8, 64], replicated, may hold values from 0 to 7
- holder_slot: int32 [2, 8, 64], replicated, may hold values from 0 to 15, as said below
- bottom_level: int32 [64, 8192], P('lat', 'lon'), may hold values from 0 to 38
- mix_class: int32 [37, 64, 8192], P(None, 'lat', 'lon'), may hold values from 0 to 7
- mix_table: float32 [8], replicated, may hold values from 0.02 to 0.4
Outputs:
- tracer_adjoint: float32 [2, 38, 64, 8192], P(None, None, 'lat', 'lon')
- velocity_adjoint: float32 [2, 38, 64, 8192], P(None, None, 'lat', 'lon')
Inputs may be any that keep to these rules, and one draw needn't show every extreme that they name: `holder_slot`: for every longitude tile, the 16 entries over all steps and bands are all different.
All inputs are finite; a program needn't handle non-finite values.
Results may differ from a plain program's by a relative error of at most 0.0014.
Values may be sent and summed in bfloat16 or wider, within the bound.
No kernel may reach another device: no remote copies, remote signals or barrier semaphores. Data moves between devices by JAX's collectives and lax.ppermute only.
A program may use at most 64 MiB of HBM per device.

v0:
```python
import jax
import jax.numpy as jnp
from jax import lax
from jax.sharding import PartitionSpec as P

STEPS = 2
ADVECT_HALF = 0.125
DIFFUSE = 0.1


def from_partner(block, axis, bit):
    count = lax.axis_size(axis)
    route = []
    for low in range(count):
        high = low | 1 << bit
        if high != low and high < count:
            route += [(low, high), (high, low)]
    return lax.ppermute(block, axis, route)


def with_halo(value, sides, width):
    for axis, dim in sides:
        devices, length = (lax.axis_size(axis), value.shape[dim])
        up = [(i, (i + 1) % devices) for i in range(devices)]
        down = [(j, i) for i, j in up]
        last = lax.slice_in_dim(value, length - width, length, axis=dim)
        first = lax.slice_in_dim(value, 0, width, axis=dim)
        before = lax.ppermute(last, axis, up)
        after = lax.ppermute(first, axis, down)
        value = jnp.concatenate([before, value, after], axis=dim)
    return value


def transpose_step(
    masked,
    east,
    west,
    north,
    south,
    tracer,
    tracer_east,
    tracer_north,
    zonal,
    zonal_west,
    meridional,
    meridional_south,
    south_open,
    kappa_below,
    kappa_above,
):
    below = jnp.concatenate([masked[:, 1:], jnp.zeros_like(masked[:, :1])], axis=1)
    above = jnp.concatenate([jnp.zeros_like(masked[:, :1]), masked[:, :-1]], axis=1)
    advect = (
        zonal * (east - masked)
        + zonal_west * (masked - west)
        + meridional * (north - masked)
        + meridional_south * (masked - south)
    )
    spread = east - masked + (west - masked) + (north - masked) + south_open * (south - masked)
    mixing = kappa_below * (below - masked) + kappa_above * (above - masked)
    result = masked + ADVECT_HALF * advect + DIFFUSE * spread + mixing
    zonal_grad = ADVECT_HALF * jnp.sum((tracer + tracer_east) * (east - masked), axis=0)
    merid_grad = ADVECT_HALF * jnp.sum((tracer + tracer_north) * (north - masked), axis=0)
    return (result, zonal_grad, merid_grad)


def fold_rows(row_block, field_kind):
    moved = row_block
    levels_bits = lax.axis_size("lon").bit_length() - 1
    for bit_index in range(levels_bits):
        if field_kind == "adjoint":
            moved = from_partner(moved.astype(jnp.bfloat16), "lon", bit_index).astype(moved.dtype)
        else:
            moved = from_partner(moved, "lon", bit_index)
    return jnp.flip(moved, axis=-1)


def shards(final_adjoint, store, holder_offset, holder_slot, bottom_level, mix_class, mix_table):
    band_index = lax.axis_index("lat")
    tile_index = lax.axis_index("lon")
    bands = lax.axis_size("lat")
    levels = final_adjoint.shape[1]
    tile_height = final_adjoint.shape[2]
    tile_width = final_adjoint.shape[3]
    top_band = band_index == bands - 1
    ocean_mask = (jnp.arange(levels, dtype=jnp.int32)[:, None, None] < bottom_level[None]).astype(
        jnp.float32
    )
    kappa = jnp.zeros(mix_class.shape, jnp.float32)
    for class_index in range(mix_table.shape[0]):
        kappa = kappa + mix_table[class_index] * (mix_class == class_index).astype(jnp.float32)
    zero_level = jnp.zeros((1, tile_height, tile_width), jnp.float32)
    kappa_below = jnp.concatenate([kappa, zero_level], axis=0)
    kappa_above = jnp.concatenate([zero_level, kappa], axis=0)
    global_rows = band_index * tile_height + jnp.arange(tile_height, dtype=jnp.int32)
    south_open = (global_rows > 0).astype(jnp.float32)[:, None]
    slot_table = lax.dynamic_index_in_dim(holder_slot, tile_index, axis=2, keepdims=False)
    offset_column = lax.dynamic_index_in_dim(holder_offset, tile_index, axis=2, keepdims=False)
    offset_steps = lax.dynamic_index_in_dim(offset_column, band_index, axis=1, keepdims=False)

    def sides(extended, mirrored):
        east = extended[..., 1:-1, 2:]
        west = extended[..., 1:-1, :-2]
        south = extended[..., :-2, 1:-1]
        north = extended[..., 2:, 1:-1]
        north = north.at[..., -1, :].set(jnp.where(top_band, mirrored, north[..., -1, :]))
        return (east, west, north, south)

    adjoint = final_adjoint
    zonal_total = jnp.zeros((levels, tile_height, tile_width), jnp.float32)
    merid_total = jnp.zeros((levels, tile_height, tile_width), jnp.float32)
    for step_index in range(STEPS - 1, -1, -1):
        request = jnp.take(store, slot_table[step_index], axis=2)
        received = lax.all_to_all(request, "lat", split_axis=2, concat_axis=2, tiled=True)
        order = (jnp.arange(bands, dtype=jnp.int32) + offset_steps[step_index]) % bands
        ordered = jnp.take(received, order, axis=2)
        trajectory = ordered.reshape(received.shape[0], received.shape[1], tile_height, tile_width)
        extended_state = with_halo(trajectory, (("lon", 3), ("lat", 2)), 1)
        top_state = jnp.stack([trajectory[0, :, -1], trajectory[1, :, -1], trajectory[3, :, -1]])
        mirror_state = fold_rows(top_state, "trajectory").astype(jnp.float32)
        masked = ocean_mask * adjoint
        extended_adjoint = with_halo(masked, (("lon", 3), ("lat", 2)), 1)
        mirror_adjoint = fold_rows(masked[:, :, -1, :], "adjoint")
        state_wide = extended_state.astype(jnp.float32)
        tracer = trajectory[0:2].astype(jnp.float32)
        zonal = trajectory[2].astype(jnp.float32)
        meridional = trajectory[3].astype(jnp.float32)
        tracer_east, tracer_west, tracer_north, tracer_south = sides(
            state_wide[0:2], mirror_state[0:2]
        )
        zonal_west = state_wide[2, :, 1:-1, :-2]
        meridional_south = state_wide[3, :, :-2, 1:-1] * south_open
        fold_velocity = jnp.where(top_band, mirror_state[2], 0.0)
        meridional_net = meridional.at[:, -1, :].set(meridional[:, -1, :] - fold_velocity)
        east, west, north, south = sides(extended_adjoint, mirror_adjoint)
        adjoint, zonal_grad, merid_grad = transpose_step(
            masked,
            east,
            west,
            north,
            south,
            tracer,
            tracer_east,
            tracer_north,
            zonal,
            zonal_west,
            meridional_net,
            meridional_south,
            south_open,
            kappa_below,
            kappa_above,
        )
        zonal_total = zonal_total + zonal_grad
        merid_total = merid_total + merid_grad
    return (adjoint, jnp.stack([zonal_total, merid_total]))


def solution(mesh):
    return jax.shard_map(
        shards,
        mesh=mesh,
        in_specs=(
            P(None, None, "lat", "lon"),
            P(None, None, None, "lat", "lon"),
            P(),
            P(),
            P("lat", "lon"),
            P(None, "lat", "lon"),
            P(),
        ),
        out_specs=(P(None, None, "lat", "lon"), P(None, None, "lat", "lon")),
        check_vma=False,
    )
```

profile of v0, /device:TPU:6, one launch (start us, length us, event | category | flops | bytes accessed | tf_op | source)
XLA Modules:
  0.0 261.9 jit_solution(3631502479113437797)
XLA Ops:
  4.9 10.2 %all-to-all-start = ((bf16[4,38,8,1,128]{4,0,1,3,2:T(4,128)(2,1)}), bf16[4,38,8,1,128]{4,0,1,3,2:T(4,128)(2,1)S(1)}, u32[]{:S(2)}, u32[]{:S(2)}) async-start(bf16[4,38,8,1,128]{4,0,1,3,2:T(4,128)(2,1)} %fusion.40), calls=%async_computation | async-start | bytes 622592 | tf_op jit(solution)/shard_map/all_to_all | solution.py:114
  15.9 10.2 %collective-permute-start = (f32[2,38,8,1]{3,2,1,0:T(8,128)S(1)}, f32[2,38,8,1]{3,2,1,0:T(8,128)S(1)}, u32[]{:S(2)}, u32[]{:S(2)}) collective-permute-start(f32[2,38,8,1]{3,2,1,0:T(8,128)S(1)} %get-tuple-element.132), channel_id=1, source_target_pairs={{8,0},{16,8},{24,16},{32,24},{40,32},{48,40},{56,48},{64,56},{72,6... | collective-permute-start | bytes 7304 | tf_op jit(solution)/shard_map/ppermute | solution.py:29
  26.1 1.9 collective-permute-start.5
  28.1 1.9 collective-permute-start.13
  35.2 5.1 %select_add_fusion = f32[37,8,128]{2,1,0:T(8,128)S(1)} fusion(s32[37,8,128]{2,1,0:T(8,128)S(1)} %copy-done.26, f32[]{:T(128)} %bitcast.28, f32[]{:T(128)} %bitcast.27, f32[]{:T(128)} %bitcast.26, f32[]{:T(128)} %bitcast.25, f32[]{:T(128)} %bitcast.24, f32[]{:T(128)} %bitcast.23, f32[]{:T(128)} %bitcast.22, f32[]{:T(128)} %bitcast.21), kind=kLoop, calls=%fused_computation.98 | loop fusion | flops 871424 | bytes 303136 | tf_op jit(solution)/shard_map/add | solution.py:91
  42.0 1.9 collective-permute-start.14
  44.6 3.1 %collective-permute-done.14 = bf16[2,38,128]{2,0,1:T(2,128)(2,1)S(1)} collective-permute-done((bf16[2,38,128]{2,0,1:T(2,128)(2,1)S(1)}, bf16[2,38,128]{2,0,1:T(2,128)(2,1)S(1)}, u32[]{:S(2)}, u32[]{:S(2)}) %collective-permute-start.14) | collective-permute-done | bytes 19488 | tf_op jit(solution)/shard_map/ppermute | solution.py:18
  50.2 4.0 %collective-permute-done.15 = bf16[2,38,128]{2,0,1:T(2,128)(2,1)S(1)} collective-permute-done((bf16[2,38,128]{2,0,1:T(2,128)(2,1)S(1)}, bf16[2,38,128]{2,0,1:T(2,128)(2,1)S(1)}, u32[]{:S(2)}, u32[]{:S(2)}) %collective-permute-start.15) | collective-permute-done | bytes 19488 | tf_op jit(solution)/shard_map/ppermute | solution.py:18
  54.2 4.7 %collective-permute-start.16 = (bf16[2,38,128]{2,0,1:T(2,128)(2,1)S(1)}, bf16[2,38,128]{2,0,1:T(2,128)(2,1)S(1)}, u32[]{:S(2)}, u32[]{:S(2)}) collective-permute-start(bf16[2,38,128]{2,0,1:T(2,128)(2,1)S(1)} %collective-permute-done.15), channel_id=1, source_target_pairs={{0,64},{64,0},{8,72},{72,8},{16,80},{80,16},{24,88},{88,24},{32,96... | collective-permute-start | bytes 58376 | tf_op jit(solution)/shard_map/ppermute | solution.py:18
  59.5 2.8 %collective-permute-start.12 = (f32[2,38,1,130]{3,2,1,0:T(1,128)S(1)}, f32[2,38,1,130]{3,2,1,0:T(1,128)S(1)}, u32[]{:S(2)}, u32[]{:S(2)}) collective-permute-start(f32[2,38,1,130]{3,2,1,0:T(1,128)S(1)} %get-tuple-element.112), channel_id=1, source_target_pairs={{1,0},{2,1},{3,2},{4,3},{5,4},{6,5},{7,6},{0,7},{9,8},{10,9},{11,1... | collective-permute-start | bytes 118568 | tf_op jit(solution)/shard_map/ppermute | solution.py:29
  63.8 3.0 %collective-permute-start.17 = (bf16[2,38,128]{2,0,1:T(2,128)(2,1)S(1)}, bf16[2,38,128]{2,0,1:T(2,128)(2,1)S(1)}, u32[]{:S(2)}, u32[]{:S(2)}) collective-permute-start(bf16[2,38,128]{2,0,1:T(2,128)(2,1)S(1)} %collective-permute-done.16), channel_id=1, source_target_pairs={{0,128},{128,0},{8,136},{136,8},{16,144},{144,16},{24,152},{152,24... | collective-permute-start | bytes 58376 | tf_op jit(solution)/shard_map/ppermute | solution.py:18
  66.8 7.3 %collective-permute-start.19 = (f32[2,38,1,130]{3,2,1,0:T(1,128)S(1)}, f32[2,38,1,130]{3,2,1,0:T(1,128)}, u32[]{:S(2)}, u32[]{:S(2)}) collective-permute-start(f32[2,38,1,130]{3,2,1,0:T(1,128)S(1)} %get-tuple-element.113), channel_id=1, source_target_pairs={{0,1},{1,2},{2,3},{3,4},{4,5},{5,6},{6,7},{7,0},{8,9},{9,10},{10,1... | collective-permute-start | bytes 118568 | tf_op jit(solution)/shard_map/ppermute | solution.py:28
  74.1 4.4 %collective-permute-start.18 = (bf16[2,38,128]{2,0,1:T(2,128)(2,1)S(1)}, bf16[2,38,128]{2,0,1:T(2,128)(2,1)S(1)}, u32[]{:S(2)}, u32[]{:S(2)}) collective-permute-start(bf16[2,38,128]{2,0,1:T(2,128)(2,1)S(1)} %collective-permute-done.17), channel_id=1, source_target_pairs={{0,256},{256,0},{8,264},{264,8},{16,272},{272,16},{24,280},{280,24... | collective-permute-start | bytes 58376 | tf_op jit(solution)/shard_map/ppermute | solution.py:18
  81.8 9.2 %all-to-all-start.1 = ((bf16[4,38,8,1,128]{4,0,1,3,2:T(4,128)(2,1)}), bf16[4,38,8,1,128]{4,0,1,3,2:T(4,128)(2,1)S(1)}, u32[]{:S(2)}, u32[]{:S(2)}) async-start(bf16[4,38,8,1,128]{4,0,1,3,2:T(4,128)(2,1)} %fusion.39), calls=%async_computation.1 | async-start | bytes 622592 | tf_op jit(solution)/shard_map/all_to_all | solution.py:114
  93.0 8.4 %all-to-all-done.1 = bf16[4,38,8,1,128]{4,0,1,3,2:T(4,128)(2,1)S(1)} async-done(((bf16[4,38,8,1,128]{4,0,1,3,2:T(4,128)(2,1)}), bf16[4,38,8,1,128]{4,0,1,3,2:T(4,128)(2,1)S(1)}, u32[]{:S(2)}, u32[]{:S(2)}) %all-to-all-start.1) | async-done | bytes 311328 | tf_op jit(solution)/shard_map/all_to_all | solution.py:114
  103.0 1.9 collective-permute-start.21
  105.0 7.5 %collective-permute-start.22 = (bf16[4,38,8,1]{3,2,1,0:T(8,128)(2,1)S(1)}, bf16[4,38,8,1]{3,2,1,0:T(8,128)(2,1)S(1)}, u32[]{:S(2)}, u32[]{:S(2)}) collective-permute-start(bf16[4,38,8,1]{3,2,1,0:T(8,128)(2,1)S(1)} %get-tuple-element.120), channel_id=1, source_target_pairs={{8,0},{16,8},{24,16},{32,24},{40,32},{48,40},{56,48},{64,56},{72,6... | collective-permute-start | bytes 7304 | tf_op jit(solution)/shard_map/ppermute | solution.py:29
  112.5 1.9 collective-permute-start.1
  114.5 7.5 %collective-permute-start.2 = (bf16[4,38,8,1]{3,2,1,0:T(8,128)(2,1)}, bf16[4,38,8,1]{3,2,1,0:T(8,128)(2,1)S(1)}, u32[]{:S(2)}, u32[]{:S(2)}) collective-permute-start(bf16[4,38,8,1]{3,2,1,0:T(8,128)(2,1)} %get-tuple-element.131), channel_id=1, source_target_pairs={{8,0},{16,8},{24,16},{32,24},{40,32},{48,40},{56,48},{64,56},{72,6... | collective-permute-start | bytes 7304 | tf_op jit(solution)/shard_map/ppermute | solution.py:29
  123.6 1.9 collective-permute-start.6
  125.6 2.4 collective-permute-start.26
  128.8 2.9 %collective-permute-start.23 = (bf16[4,38,1,130]{3,2,1,0:T(2,128)(2,1)S(1)}, bf16[4,38,1,130]{3,2,1,0:T(2,128)(2,1)S(1)}, u32[]{:S(2)}, u32[]{:S(2)}) collective-permute-start(bf16[4,38,1,130]{3,2,1,0:T(2,128)(2,1)S(1)} %get-tuple-element.106), channel_id=1, source_target_pairs={{0,1},{1,2},{2,3},{3,4},{4,5},{5,6},{6,7},{7,0},{8,9},{9,10},{10,1... | collective-permute-start | bytes 118568 | tf_op jit(solution)/shard_map/ppermute | solution.py:28
  131.7 2.9 %collective-permute-start.24 = (bf16[4,38,1,130]{3,2,1,0:T(2,128)(2,1)S(1)}, bf16[4,38,1,130]{3,2,1,0:T(2,128)(2,1)S(1)}, u32[]{:S(2)}, u32[]{:S(2)}) collective-permute-start(bf16[4,38,1,130]{3,2,1,0:T(2,128)(2,1)S(1)} %get-tuple-element.107), channel_id=1, source_target_pairs={{1,0},{2,1},{3,2},{4,3},{5,4},{6,5},{7,6},{0,7},{9,8},{10,9},{11,1... | collective-permute-start | bytes 118568 | tf_op jit(solution)/shard_map/ppermute | solution.py:29
  135.4 8.9 %collective-permute-start.3 = (bf16[4,38,1,130]{3,2,1,0:T(2,128)(2,1)S(1)}, bf16[4,38,1,130]{3,2,1,0:T(2,128)(2,1)S(1)}, u32[]{:S(2)}, u32[]{:S(2)}) collective-permute-start(bf16[4,38,1,130]{3,2,1,0:T(2,128)(2,1)S(1)} %get-tuple-element.110), channel_id=1, source_target_pairs={{0,1},{1,2},{2,3},{3,4},{4,5},{5,6},{6,7},{7,0},{8,9},{9,10},{10,1... | collective-permute-start | bytes 118568 | tf_op jit(solution)/shard_map/ppermute | solution.py:28
  144.4 1.9 collective-permute-start.4
  146.3 1.9 collective-permute-start.7
  148.2 3.9 %collective-permute-start.27 = (bf16[3,38,128]{2,0,1:T(4,128)(2,1)S(1)}, bf16[3,38,128]{2,0,1:T(4,128)(2,1)S(1)}, u32[]{:S(2)}, u32[]{:S(2)}) collective-permute-start(bf16[3,38,128]{2,0,1:T(4,128)(2,1)S(1)} %collective-permute-done.26), channel_id=1, source_target_pairs={{0,16},{16,0},{8,24},{24,8},{32,48},{48,32},{40,56},{56,40},{64,80... | collective-permute-start | bytes 87560 | tf_op jit(solution)/shard_map/ppermute | solution.py:18
  153.3 6.6 %collective-permute-done.4 = bf16[4,38,1,130]{3,2,1,0:T(2,128)(2,1)S(1)} collective-permute-done((bf16[4,38,1,130]{3,2,1,0:T(2,128)(2,1)S(1)}, bf16[4,38,1,130]{3,2,1,0:T(2,128)(2,1)S(1)}, u32[]{:S(2)}, u32[]{:S(2)}) %collective-permute-start.4) | collective-permute-done | bytes 39552 | tf_op jit(solution)/shard_map/ppermute | solution.py:29
  164.6 4.8 %collective-permute-start.28 = (bf16[3,38,128]{2,0,1:T(4,128)(2,1)S(1)}, bf16[3,38,128]{2,0,1:T(4,128)(2,1)S(1)}, u32[]{:S(2)}, u32[]{:S(2)}) collective-permute-start(bf16[3,38,128]{2,0,1:T(4,128)(2,1)S(1)} %collective-permute-done.27), channel_id=1, source_target_pairs={{0,32},{32,0},{8,40},{40,8},{16,48},{48,16},{24,56},{56,24},{64,96... | collective-permute-start | bytes 87560 | tf_op jit(solution)/shard_map/ppermute | solution.py:18
  172.1 7.8 %collective-permute-start.29 = (bf16[3,38,128]{2,0,1:T(4,128)(2,1)S(1)}, bf16[3,38,128]{2,0,1:T(4,128)(2,1)S(1)}, u32[]{:S(2)}, u32[]{:S(2)}) collective-permute-start(bf16[3,38,128]{2,0,1:T(4,128)(2,1)S(1)} %collective-permute-done.28), channel_id=1, source_target_pairs={{0,64},{64,0},{8,72},{72,8},{16,80},{80,16},{24,88},{88,24},{32,96... | collective-permute-start | bytes 87560 | tf_op jit(solution)/shard_map/ppermute | solution.py:18
  182.0 3.9 %collective-permute-start.30 = (bf16[3,38,128]{2,0,1:T(4,128)(2,1)S(1)}, bf16[3,38,128]{2,0,1:T(4,128)(2,1)}, u32[]{:S(2)}, u32[]{:S(2)}) collective-permute-start(bf16[3,38,128]{2,0,1:T(4,128)(2,1)S(1)} %collective-permute-done.29), channel_id=1, source_target_pairs={{0,128},{128,0},{8,136},{136,8},{16,144},{144,16},{24,152},{152,24... | collective-permute-start | bytes 87560 | tf_op jit(solution)/shard_map/ppermute | solution.py:18
  186.0 2.2 collective-permute-start.11
  188.9 4.6 %collective-permute-start.31 = (bf16[3,38,128]{2,0,1:T(4,128)(2,1)}, bf16[3,38,128]{2,0,1:T(4,128)(2,1)}, u32[]{:S(2)}, u32[]{:S(2)}) collective-permute-start(bf16[3,38,128]{2,0,1:T(4,128)(2,1)} %collective-permute-done.30), channel_id=1, source_target_pairs={{0,256},{256,0},{8,264},{264,8},{16,272},{272,16},{24,280},{280,24... | collective-permute-start | bytes 87560 | tf_op jit(solution)/shard_map/ppermute | solution.py:18
  194.7 2.0 fusion.31
  202.0 4.0 %collective-permute-start.20 = (f32[2,38,8,1]{3,2,1,0:T(8,128)}, f32[2,38,8,1]{3,2,1,0:T(8,128)S(1)}, u32[]{:S(2)}, u32[]{:S(2)}) collective-permute-start(f32[2,38,8,1]{3,2,1,0:T(8,128)} %get-tuple-element.121), channel_id=1, source_target_pairs={{8,0},{16,8},{24,16},{32,24},{40,32},{48,40},{56,48},{64,56},{72,6... | collective-permute-start | bytes 7304 | tf_op jit(solution)/shard_map/ppermute | solution.py:29
  206.0 1.9 collective-permute-start.25
  208.0 2.0 collective-permute-start.34
  210.6 3.3 %collective-permute-done.34 = bf16[2,38,128]{2,0,1:T(2,128)(2,1)} collective-permute-done((bf16[2,38,128]{2,0,1:T(2,128)(2,1)}, bf16[2,38,128]{2,0,1:T(2,128)(2,1)}, u32[]{:S(2)}, u32[]{:S(2)}) %collective-permute-start.34) | collective-permute-done | bytes 19488 | tf_op jit(solution)/shard_map/ppermute | solution.py:18
  218.7 2.1 collective-permute-done.35
  220.8 4.3 %collective-permute-start.36 = (bf16[2,38,128]{2,0,1:T(2,128)(2,1)}, bf16[2,38,128]{2,0,1:T(2,128)(2,1)S(1)}, u32[]{:S(2)}, u32[]{:S(2)}) collective-permute-start(bf16[2,38,128]{2,0,1:T(2,128)(2,1)} %collective-permute-done.35), channel_id=1, source_target_pairs={{0,64},{64,0},{8,72},{72,8},{16,80},{80,16},{24,88},{88,24},{32,96... | collective-permute-start | bytes 58376 | tf_op jit(solution)/shard_map/ppermute | solution.py:18
  225.1 2.3 pad_maximum_fusion.25
  227.4 2.0 collective-permute-start.32
  230.9 2.5 collective-permute-start.37
  233.4 2.2 fusion.1
  239.0 9.9 %collective-permute-start.39 = (f32[2,38,1,130]{3,2,1,0:T(1,128)}, f32[2,38,1,130]{3,2,1,0:T(1,128)}, u32[]{:S(2)}, u32[]{:S(2)}) collective-permute-start(f32[2,38,1,130]{3,2,1,0:T(1,128)} %get-tuple-element.109), channel_id=1, source_target_pairs={{0,1},{1,2},{2,3},{3,4},{4,5},{5,6},{6,7},{7,0},{8,9},{9,10},{10,1... | collective-permute-start | bytes 118568 | tf_op jit(solution)/shard_map/ppermute | solution.py:28
  249.0 2.5 collective-permute-start.38
  253.0 2.8 %collective-permute-done.38 = bf16[2,38,128]{2,0,1:T(2,128)(2,1)S(1)} collective-permute-done((bf16[2,38,128]{2,0,1:T(2,128)(2,1)}, bf16[2,38,128]{2,0,1:T(2,128)(2,1)S(1)}, u32[]{:S(2)}, u32[]{:S(2)}) %collective-permute-start.38) | collective-permute-done | bytes 19488 | tf_op jit(solution)/shard_map/ppermute | solution.py:18
  259.6 2.3 fusion.15
  (189 shorter events, 60.3 us)
Async XLA Ops:
  4.9 76.3 %all-to-all-start = ((bf16[4,38,8,1,128]{4,0,1,3,2:T(4,128)(2,1)}), bf16[4,38,8,1,128]{4,0,1,3,2:T(4,128)(2,1)S(1)}, u32[]{:S(2)}, u32[]{:S(2)}) async-start(bf16[4,38,8,1,128]{4,0,1,3,2:T(4,128)(2,1)} %fusion.40), calls=%async_computation | async-start | bytes 622592 | tf_op jit(solution)/shard_map/all_to_all | solution.py:114
  15.9 43.0 %collective-permute-start = (f32[2,38,8,1]{3,2,1,0:T(8,128)S(1)}, f32[2,38,8,1]{3,2,1,0:T(8,128)S(1)}, u32[]{:S(2)}, u32[]{:S(2)}) collective-permute-start(f32[2,38,8,1]{3,2,1,0:T(8,128)S(1)} %get-tuple-element.132), channel_id=1, source_target_pairs={{8,0},{16,8},{24,16},{32,24},{40,32},{48,40},{56,48},{64,56},{72,6... | collective-permute-start | bytes 7304 | tf_op jit(solution)/shard_map/ppermute | solution.py:29
  26.1 32.9 %collective-permute-start.5 = (f32[2,38,8,1]{3,2,1,0:T(8,128)S(1)}, f32[2,38,8,1]{3,2,1,0:T(8,128)S(1)}, u32[]{:S(2)}, u32[]{:S(2)}) collective-permute-start(f32[2,38,8,1]{3,2,1,0:T(8,128)S(1)} %get-tuple-element.133), channel_id=1, source_target_pairs={{0,8},{8,16},{16,24},{24,32},{32,40},{40,48},{48,56},{56,64},{64,7... | collective-permute-start | bytes 7304 | tf_op jit(solution)/shard_map/ppermute | solution.py:28
  28.1 13.9 %collective-permute-start.13 = (bf16[2,38,128]{2,0,1:T(2,128)(2,1)S(1)}, bf16[2,38,128]{2,0,1:T(2,128)(2,1)S(1)}, u32[]{:S(2)}, u32[]{:S(2)}) collective-permute-start(bf16[2,38,128]{2,0,1:T(2,128)(2,1)S(1)} %bitcast.147), channel_id=1, source_target_pairs={{0,8},{8,0},{16,24},{24,16},{32,40},{40,32},{48,56},{56,48},{64,72... | collective-permute-start | bytes 58376 | tf_op jit(solution)/shard_map/ppermute | solution.py:18
  42.0 5.7 %collective-permute-start.14 = (bf16[2,38,128]{2,0,1:T(2,128)(2,1)S(1)}, bf16[2,38,128]{2,0,1:T(2,128)(2,1)S(1)}, u32[]{:S(2)}, u32[]{:S(2)}) collective-permute-start(bf16[2,38,128]{2,0,1:T(2,128)(2,1)S(1)} %collective-permute-done.13), channel_id=1, source_target_pairs={{0,16},{16,0},{8,24},{24,8},{32,48},{48,32},{40,56},{56,40},{64,80... | collective-permute-start | bytes 58376 | tf_op jit(solution)/shard_map/ppermute | solution.py:18
  47.7 6.6 %collective-permute-start.15 = (bf16[2,38,128]{2,0,1:T(2,128)(2,1)S(1)}, bf16[2,38,128]{2,0,1:T(2,128)(2,1)S(1)}, u32[]{:S(2)}, u32[]{:S(2)}) collective-permute-start(bf16[2,38,128]{2,0,1:T(2,128)(2,1)S(1)} %collective-permute-done.14), channel_id=1, source_target_pairs={{0,32},{32,0},{8,40},{40,8},{16,48},{48,16},{24,56},{56,24},{64,96... | collective-permute-start | bytes 58376 | tf_op jit(solution)/shard_map/ppermute | solution.py:18
  54.2 9.6 %collective-permute-start.16 = (bf16[2,38,128]{2,0,1:T(2,128)(2,1)S(1)}, bf16[2,38,128]{2,0,1:T(2,128)(2,1)S(1)}, u32[]{:S(2)}, u32[]{:S(2)}) collective-permute-start(bf16[2,38,128]{2,0,1:T(2,128)(2,1)S(1)} %collective-permute-done.15), channel_id=1, source_target_pairs={{0,64},{64,0},{8,72},{72,8},{16,80},{80,16},{24,88},{88,24},{32,96... | collective-permute-start | bytes 58376 | tf_op jit(solution)/shard_map/ppermute | solution.py:18
  59.5 19.0 %collective-permute-start.12 = (f32[2,38,1,130]{3,2,1,0:T(1,128)S(1)}, f32[2,38,1,130]{3,2,1,0:T(1,128)S(1)}, u32[]{:S(2)}, u32[]{:S(2)}) collective-permute-start(f32[2,38,1,130]{3,2,1,0:T(1,128)S(1)} %get-tuple-element.112), channel_id=1, source_target_pairs={{1,0},{2,1},{3,2},{4,3},{5,4},{6,5},{7,6},{0,7},{9,8},{10,9},{11,1... | collective-permute-start | bytes 118568 | tf_op jit(solution)/shard_map/ppermute | solution.py:29
  63.8 10.3 %collective-permute-start.17 = (bf16[2,38,128]{2,0,1:T(2,128)(2,1)S(1)}, bf16[2,38,128]{2,0,1:T(2,128)(2,1)S(1)}, u32[]{:S(2)}, u32[]{:S(2)}) collective-permute-start(bf16[2,38,128]{2,0,1:T(2,128)(2,1)S(1)} %collective-permute-done.16), channel_id=1, source_target_pairs={{0,128},{128,0},{8,136},{136,8},{16,144},{144,16},{24,152},{152,24... | collective-permute-start | bytes 58376 | tf_op jit(solution)/shard_map/ppermute | solution.py:18
  66.8 127.2 %collective-permute-start.19 = (f32[2,38,1,130]{3,2,1,0:T(1,128)S(1)}, f32[2,38,1,130]{3,2,1,0:T(1,128)}, u32[]{:S(2)}, u32[]{:S(2)}) collective-permute-start(f32[2,38,1,130]{3,2,1,0:T(1,128)S(1)} %get-tuple-element.113), channel_id=1, source_target_pairs={{0,1},{1,2},{2,3},{3,4},{4,5},{5,6},{6,7},{7,0},{8,9},{9,10},{10,1... | collective-permute-start | bytes 118568 | tf_op jit(solution)/shard_map/ppermute | solution.py:28
  74.1 6.6 %collective-permute-start.18 = (bf16[2,38,128]{2,0,1:T(2,128)(2,1)S(1)}, bf16[2,38,128]{2,0,1:T(2,128)(2,1)S(1)}, u32[]{:S(2)}, u32[]{:S(2)}) collective-permute-start(bf16[2,38,128]{2,0,1:T(2,128)(2,1)S(1)} %collective-permute-done.17), channel_id=1, source_target_pairs={{0,256},{256,0},{8,264},{264,8},{16,272},{272,16},{24,280},{280,24... | collective-permute-start | bytes 58376 | tf_op jit(solution)/shard_map/ppermute | solution.py:18
  81.8 19.6 %all-to-all-start.1 = ((bf16[4,38,8,1,128]{4,0,1,3,2:T(4,128)(2,1)}), bf16[4,38,8,1,128]{4,0,1,3,2:T(4,128)(2,1)S(1)}, u32[]{:S(2)}, u32[]{:S(2)}) async-start(bf16[4,38,8,1,128]{4,0,1,3,2:T(4,128)(2,1)} %fusion.39), calls=%async_computation.1 | async-start | bytes 622592 | tf_op jit(solution)/shard_map/all_to_all | solution.py:114
  102.9 19.1 %copy-start.11 = (bf16[4,38,8,1,128]{4,2,1,3,0:T(8,128)(2,1)}, bf16[4,38,8,1,128]{4,2,1,3,0:T(8,128)(2,1)S(1)}, u32[]{:S(2)}) copy-start(bf16[4,38,8,1,128]{4,2,1,3,0:T(8,128)(2,1)S(1)} %bitcast_select_fusion.2) | copy-start | bytes 933892
  103.0 20.4 %copy-start.9 = (bf16[4,38,8,1,128]{4,2,1,0,3:T(8,128)(2,1)}, bf16[4,38,8,1,128]{4,2,1,0,3:T(8,128)(2,1)S(1)}, u32[]{:S(2)}) copy-start(bf16[4,38,8,1,128]{4,2,1,0,3:T(8,128)(2,1)S(1)} %bitcast_select_fusion) | copy-start | bytes 933892
  103.0 20.6 %collective-permute-start.21 = (bf16[4,38,8,1]{3,2,1,0:T(8,128)(2,1)S(1)}, bf16[4,38,8,1]{3,2,1,0:T(8,128)(2,1)S(1)}, u32[]{:S(2)}, u32[]{:S(2)}) collective-permute-start(bf16[4,38,8,1]{3,2,1,0:T(8,128)(2,1)S(1)} %get-tuple-element.119), channel_id=1, source_target_pairs={{0,8},{8,16},{16,24},{24,32},{32,40},{40,48},{48,56},{56,64},{64,7... | collective-permute-start | bytes 7304 | tf_op jit(solution)/shard_map/ppermute | solution.py:28
  105.0 20.6 %collective-permute-start.22 = (bf16[4,38,8,1]{3,2,1,0:T(8,128)(2,1)S(1)}, bf16[4,38,8,1]{3,2,1,0:T(8,128)(2,1)S(1)}, u32[]{:S(2)}, u32[]{:S(2)}) collective-permute-start(bf16[4,38,8,1]{3,2,1,0:T(8,128)(2,1)S(1)} %get-tuple-element.120), channel_id=1, source_target_pairs={{8,0},{16,8},{24,16},{32,24},{40,32},{48,40},{56,48},{64,56},{72,6... | collective-permute-start | bytes 7304 | tf_op jit(solution)/shard_map/ppermute | solution.py:29
  112.5 16.2 %collective-permute-start.1 = (bf16[4,38,8,1]{3,2,1,0:T(8,128)(2,1)S(1)}, bf16[4,38,8,1]{3,2,1,0:T(8,128)(2,1)S(1)}, u32[]{:S(2)}, u32[]{:S(2)}) collective-permute-start(bf16[4,38,8,1]{3,2,1,0:T(8,128)(2,1)S(1)} %get-tuple-element.130), channel_id=1, source_target_pairs={{0,8},{8,16},{16,24},{24,32},{32,40},{40,48},{48,56},{56,64},{64,7... | collective-permute-start | bytes 7304 | tf_op jit(solution)/shard_map/ppermute | solution.py:28
  114.5 17.2 %collective-permute-start.2 = (bf16[4,38,8,1]{3,2,1,0:T(8,128)(2,1)}, bf16[4,38,8,1]{3,2,1,0:T(8,128)(2,1)S(1)}, u32[]{:S(2)}, u32[]{:S(2)}) collective-permute-start(bf16[4,38,8,1]{3,2,1,0:T(8,128)(2,1)} %get-tuple-element.131), channel_id=1, source_target_pairs={{8,0},{16,8},{24,16},{32,24},{40,32},{48,40},{56,48},{64,56},{72,6... | collective-permute-start | bytes 7304 | tf_op jit(solution)/shard_map/ppermute | solution.py:29
  123.6 11.8 %collective-permute-start.6 = (bf16[3,38,128]{2,0,1:T(4,128)(2,1)S(1)}, bf16[3,38,128]{2,0,1:T(4,128)(2,1)S(1)}, u32[]{:S(2)}, u32[]{:S(2)}) collective-permute-start(bf16[3,38,128]{2,0,1:T(4,128)(2,1)S(1)} %pad_maximum_fusion.37), channel_id=1, source_target_pairs={{0,8},{8,0},{16,24},{24,16},{32,40},{40,32},{48,56},{56,48},{64,72... | collective-permute-start | bytes 87560 | tf_op jit(solution)/shard_map/ppermute | solution.py:18
  125.6 18.8 %collective-permute-start.26 = (bf16[3,38,128]{2,0,1:T(4,128)(2,1)S(1)}, bf16[3,38,128]{2,0,1:T(4,128)(2,1)S(1)}, u32[]{:S(2)}, u32[]{:S(2)}) collective-permute-start(bf16[3,38,128]{2,0,1:T(4,128)(2,1)S(1)} %pad_maximum_fusion.38), channel_id=1, source_target_pairs={{0,8},{8,0},{16,24},{24,16},{32,40},{40,32},{48,56},{56,48},{64,72... | collective-permute-start | bytes 87560 | tf_op jit(solution)/shard_map/ppermute | solution.py:18
  128.8 17.5 %collective-permute-start.23 = (bf16[4,38,1,130]{3,2,1,0:T(2,128)(2,1)S(1)}, bf16[4,38,1,130]{3,2,1,0:T(2,128)(2,1)S(1)}, u32[]{:S(2)}, u32[]{:S(2)}) collective-permute-start(bf16[4,38,1,130]{3,2,1,0:T(2,128)(2,1)S(1)} %get-tuple-element.106), channel_id=1, source_target_pairs={{0,1},{1,2},{2,3},{3,4},{4,5},{5,6},{6,7},{7,0},{8,9},{9,10},{10,1... | collective-permute-start | bytes 118568 | tf_op jit(solution)/shard_map/ppermute | solution.py:28
  131.7 16.5 %collective-permute-start.24 = (bf16[4,38,1,130]{3,2,1,0:T(2,128)(2,1)S(1)}, bf16[4,38,1,130]{3,2,1,0:T(2,128)(2,1)S(1)}, u32[]{:S(2)}, u32[]{:S(2)}) collective-permute-start(bf16[4,38,1,130]{3,2,1,0:T(2,128)(2,1)S(1)} %get-tuple-element.107), channel_id=1, source_target_pairs={{1,0},{2,1},{3,2},{4,3},{5,4},{6,5},{7,6},{0,7},{9,8},{10,9},{11,1... | collective-permute-start | bytes 118568 | tf_op jit(solution)/shard_map/ppermute | solution.py:29
  135.4 17.9 %collective-permute-start.3 = (bf16[4,38,1,130]{3,2,1,0:T(2,128)(2,1)S(1)}, bf16[4,38,1,130]{3,2,1,0:T(2,128)(2,1)S(1)}, u32[]{:S(2)}, u32[]{:S(2)}) collective-permute-start(bf16[4,38,1,130]{3,2,1,0:T(2,128)(2,1)S(1)} %get-tuple-element.110), channel_id=1, source_target_pairs={{0,1},{1,2},{2,3},{3,4},{4,5},{5,6},{6,7},{7,0},{8,9},{9,10},{10,1... | collective-permute-start | bytes 118568 | tf_op jit(solution)/shard_map/ppermute | solution.py:28
  144.4 15.5 %collective-permute-start.4 = (bf16[4,38,1,130]{3,2,1,0:T(2,128)(2,1)S(1)}, bf16[4,38,1,130]{3,2,1,0:T(2,128)(2,1)S(1)}, u32[]{:S(2)}, u32[]{:S(2)}) collective-permute-start(bf16[4,38,1,130]{3,2,1,0:T(2,128)(2,1)S(1)} %get-tuple-element.111), channel_id=1, source_target_pairs={{1,0},{2,1},{3,2},{4,3},{5,4},{6,5},{7,6},{0,7},{9,8},{10,9},{11,1... | collective-permute-start | bytes 118568 | tf_op jit(solution)/shard_map/ppermute | solution.py:29
  146.3 15.6 %collective-permute-start.7 = (bf16[3,38,128]{2,0,1:T(4,128)(2,1)S(1)}, bf16[3,38,128]{2,0,1:T(4,128)(2,1)S(1)}, u32[]{:S(2)}, u32[]{:S(2)}) collective-permute-start(bf16[3,38,128]{2,0,1:T(4,128)(2,1)S(1)} %collective-permute-done.6), channel_id=1, source_target_pairs={{0,16},{16,0},{8,24},{24,8},{32,48},{48,32},{40,56},{56,40},{64,80... | collective-permute-start | bytes 87560 | tf_op jit(solution)/shard_map/ppermute | solution.py:18
  148.2 16.3 %collective-permute-start.27 = (bf16[3,38,128]{2,0,1:T(4,128)(2,1)S(1)}, bf16[3,38,128]{2,0,1:T(4,128)(2,1)S(1)}, u32[]{:S(2)}, u32[]{:S(2)}) collective-permute-start(bf16[3,38,128]{2,0,1:T(4,128)(2,1)S(1)} %collective-permute-done.26), channel_id=1, source_target_pairs={{0,16},{16,0},{8,24},{24,8},{32,48},{48,32},{40,56},{56,40},{64,80... | collective-permute-start | bytes 87560 | tf_op jit(solution)/shard_map/ppermute | solution.py:18
  153.3 28.6 %copy-start = (bf16[4,38,1,130]{3,2,1,0:T(2,128)(2,1)}, bf16[4,38,1,130]{3,2,1,0:T(2,128)(2,1)S(1)}, u32[]{:S(2)}) copy-start(bf16[4,38,1,130]{3,2,1,0:T(2,128)(2,1)S(1)} %collective-permute-done.3) | copy-start | bytes 118564
  159.9 22.0 %copy-start.2 = (bf16[4,38,1,130]{3,2,1,0:T(2,128)(2,1)}, bf16[4,38,1,130]{3,2,1,0:T(2,128)(2,1)S(1)}, u32[]{:S(2)}) copy-start(bf16[4,38,1,130]{3,2,1,0:T(2,128)(2,1)S(1)} %collective-permute-done.4) | copy-start | bytes 118564
  161.9 7.5 %collective-permute-start.8 = (bf16[3,38,128]{2,0,1:T(4,128)(2,1)S(1)}, bf16[3,38,128]{2,0,1:T(4,128)(2,1)S(1)}, u32[]{:S(2)}, u32[]{:S(2)}) collective-permute-start(bf16[3,38,128]{2,0,1:T(4,128)(2,1)S(1)} %collective-permute-done.7), channel_id=1, source_target_pairs={{0,32},{32,0},{8,40},{40,8},{16,48},{48,16},{24,56},{56,24},{64,96... | collective-permute-start | bytes 87560 | tf_op jit(solution)/shard_map/ppermute | solution.py:18
  164.6 7.5 %collective-permute-start.28 = (bf16[3,38,128]{2,0,1:T(4,128)(2,1)S(1)}, bf16[3,38,128]{2,0,1:T(4,128)(2,1)S(1)}, u32[]{:S(2)}, u32[]{:S(2)}) collective-permute-start(bf16[3,38,128]{2,0,1:T(4,128)(2,1)S(1)} %collective-permute-done.27), channel_id=1, source_target_pairs={{0,32},{32,0},{8,40},{40,8},{16,48},{48,16},{24,56},{56,24},{64,96... | collective-permute-start | bytes 87560 | tf_op jit(solution)/shard_map/ppermute | solution.py:18
  169.4 10.5 %collective-permute-start.9 = (bf16[3,38,128]{2,0,1:T(4,128)(2,1)S(1)}, bf16[3,38,128]{2,0,1:T(4,128)(2,1)S(1)}, u32[]{:S(2)}, u32[]{:S(2)}) collective-permute-start(bf16[3,38,128]{2,0,1:T(4,128)(2,1)S(1)} %collective-permute-done.8), channel_id=1, source_target_pairs={{0,64},{64,0},{8,72},{72,8},{16,80},{80,16},{24,88},{88,24},{32,96... | collective-permute-start | bytes 87560 | tf_op jit(solution)/shard_map/ppermute | solution.py:18
  172.1 9.9 %collective-permute-start.29 = (bf16[3,38,128]{2,0,1:T(4,128)(2,1)S(1)}, bf16[3,38,128]{2,0,1:T(4,128)(2,1)S(1)}, u32[]{:S(2)}, u32[]{:S(2)}) collective-permute-start(bf16[3,38,128]{2,0,1:T(4,128)(2,1)S(1)} %collective-permute-done.28), channel_id=1, source_target_pairs={{0,64},{64,0},{8,72},{72,8},{16,80},{80,16},{24,88},{88,24},{32,96... | collective-permute-start | bytes 87560 | tf_op jit(solution)/shard_map/ppermute | solution.py:18
  179.9 6.0 %collective-permute-start.10 = (bf16[3,38,128]{2,0,1:T(4,128)(2,1)S(1)}, bf16[3,38,128]{2,0,1:T(4,128)(2,1)S(1)}, u32[]{:S(2)}, u32[]{:S(2)}) collective-permute-start(bf16[3,38,128]{2,0,1:T(4,128)(2,1)S(1)} %collective-permute-done.9), channel_id=1, source_target_pairs={{0,128},{128,0},{8,136},{136,8},{16,144},{144,16},{24,152},{152,24... | collective-permute-start | bytes 87560 | tf_op jit(solution)/shard_map/ppermute | solution.py:18
  182.0 6.9 %collective-permute-start.30 = (bf16[3,38,128]{2,0,1:T(4,128)(2,1)S(1)}, bf16[3,38,128]{2,0,1:T(4,128)(2,1)}, u32[]{:S(2)}, u32[]{:S(2)}) collective-permute-start(bf16[3,38,128]{2,0,1:T(4,128)(2,1)S(1)} %collective-permute-done.29), channel_id=1, source_target_pairs={{0,128},{128,0},{8,136},{136,8},{16,144},{144,16},{24,152},{152,24... | collective-permute-start | bytes 87560 | tf_op jit(solution)/shard_map/ppermute | solution.py:18
  186.0 7.5 %collective-permute-start.11 = (bf16[3,38,128]{2,0,1:T(4,128)(2,1)S(1)}, bf16[3,38,128]{2,0,1:T(4,128)(2,1)S(1)}, u32[]{:S(2)}, u32[]{:S(2)}) collective-permute-start(bf16[3,38,128]{2,0,1:T(4,128)(2,1)S(1)} %collective-permute-done.10), channel_id=1, source_target_pairs={{0,256},{256,0},{8,264},{264,8},{16,272},{272,16},{24,280},{280,24... | collective-permute-start | bytes 87560 | tf_op jit(solution)/shard_map/ppermute | solution.py:18
  188.9 12.2 %collective-permute-start.31 = (bf16[3,38,128]{2,0,1:T(4,128)(2,1)}, bf16[3,38,128]{2,0,1:T(4,128)(2,1)}, u32[]{:S(2)}, u32[]{:S(2)}) collective-permute-start(bf16[3,38,128]{2,0,1:T(4,128)(2,1)} %collective-permute-done.30), channel_id=1, source_target_pairs={{0,256},{256,0},{8,264},{264,8},{16,272},{272,16},{24,280},{280,24... | collective-permute-start | bytes 87560 | tf_op jit(solution)/shard_map/ppermute | solution.py:18
  198.3 9.7 %collective-permute-start.33 = (bf16[2,38,128]{2,0,1:T(2,128)(2,1)}, bf16[2,38,128]{2,0,1:T(2,128)(2,1)}, u32[]{:S(2)}, u32[]{:S(2)}) collective-permute-start(bf16[2,38,128]{2,0,1:T(2,128)(2,1)} %bitcast.142), channel_id=1, source_target_pairs={{0,8},{8,0},{16,24},{24,16},{32,40},{40,32},{48,56},{56,48},{64,72... | collective-permute-start | bytes 58376 | tf_op jit(solution)/shard_map/ppermute | solution.py:18
  202.0 23.0 %collective-permute-start.20 = (f32[2,38,8,1]{3,2,1,0:T(8,128)}, f32[2,38,8,1]{3,2,1,0:T(8,128)S(1)}, u32[]{:S(2)}, u32[]{:S(2)}) collective-permute-start(f32[2,38,8,1]{3,2,1,0:T(8,128)} %get-tuple-element.121), channel_id=1, source_target_pairs={{8,0},{16,8},{24,16},{32,24},{40,32},{48,40},{56,48},{64,56},{72,6... | collective-permute-start | bytes 7304 | tf_op jit(solution)/shard_map/ppermute | solution.py:29
  206.0 19.1 %collective-permute-start.25 = (f32[2,38,8,1]{3,2,1,0:T(8,128)}, f32[2,38,8,1]{3,2,1,0:T(8,128)}, u32[]{:S(2)}, u32[]{:S(2)}) collective-permute-start(f32[2,38,8,1]{3,2,1,0:T(8,128)} %get-tuple-element.122), channel_id=1, source_target_pairs={{0,8},{8,16},{16,24},{24,32},{32,40},{40,48},{48,56},{56,64},{64,7... | collective-permute-start | bytes 7304 | tf_op jit(solution)/shard_map/ppermute | solution.py:28
  208.0 6.0 %collective-permute-start.34 = (bf16[2,38,128]{2,0,1:T(2,128)(2,1)}, bf16[2,38,128]{2,0,1:T(2,128)(2,1)}, u32[]{:S(2)}, u32[]{:S(2)}) collective-permute-start(bf16[2,38,128]{2,0,1:T(2,128)(2,1)} %collective-permute-done.33), channel_id=1, source_target_pairs={{0,16},{16,0},{8,24},{24,8},{32,48},{48,32},{40,56},{56,40},{64,80... | collective-permute-start | bytes 58376 | tf_op jit(solution)/shard_map/ppermute | solution.py:18
  213.9 6.9 %collective-permute-start.35 = (bf16[2,38,128]{2,0,1:T(2,128)(2,1)}, bf16[2,38,128]{2,0,1:T(2,128)(2,1)}, u32[]{:S(2)}, u32[]{:S(2)}) collective-permute-start(bf16[2,38,128]{2,0,1:T(2,128)(2,1)} %collective-permute-done.34), channel_id=1, source_target_pairs={{0,32},{32,0},{8,40},{40,8},{16,48},{48,16},{24,56},{56,24},{64,96... | collective-permute-start | bytes 58376 | tf_op jit(solution)/shard_map/ppermute | solution.py:18
  218.7 14.7 %copy-start.5 = (f32[2,38,8,128]{3,2,1,0:T(8,128)S(1)}, f32[2,38,8,128]{3,2,1,0:T(8,128)}, u32[]{:S(2)}) copy-start(f32[2,38,8,128]{3,2,1,0:T(8,128)} %copy-done.4) | copy-start | bytes 933892
  218.7 14.8 %copy-start.12 = (bf16[4,38,8,1,128]{4,2,1,3,0:T(8,128)(2,1)S(1)}, bf16[4,38,8,1,128]{4,2,1,3,0:T(8,128)(2,1)}, u32[]{:S(2)}) copy-start(bf16[4,38,8,1,128]{4,2,1,3,0:T(8,128)(2,1)} %copy-done.11) | copy-start | bytes 933892
  220.8 10.1 %collective-permute-start.36 = (bf16[2,38,128]{2,0,1:T(2,128)(2,1)}, bf16[2,38,128]{2,0,1:T(2,128)(2,1)S(1)}, u32[]{:S(2)}, u32[]{:S(2)}) collective-permute-start(bf16[2,38,128]{2,0,1:T(2,128)(2,1)} %collective-permute-done.35), channel_id=1, source_target_pairs={{0,64},{64,0},{8,72},{72,8},{16,80},{80,16},{24,88},{88,24},{32,96... | collective-permute-start | bytes 58376 | tf_op jit(solution)/shard_map/ppermute | solution.py:18
  227.4 24.1 %collective-permute-start.32 = (f32[2,38,1,130]{3,2,1,0:T(1,128)}, f32[2,38,1,130]{3,2,1,0:T(1,128)S(1)}, u32[]{:S(2)}, u32[]{:S(2)}) collective-permute-start(f32[2,38,1,130]{3,2,1,0:T(1,128)} %get-tuple-element.108), channel_id=1, source_target_pairs={{1,0},{2,1},{3,2},{4,3},{5,4},{6,5},{7,6},{0,7},{9,8},{10,9},{11,1... | collective-permute-start | bytes 118568 | tf_op jit(solution)/shard_map/ppermute | solution.py:29
  230.9 18.1 %collective-permute-start.37 = (bf16[2,38,128]{2,0,1:T(2,128)(2,1)S(1)}, bf16[2,38,128]{2,0,1:T(2,128)(2,1)}, u32[]{:S(2)}, u32[]{:S(2)}) collective-permute-start(bf16[2,38,128]{2,0,1:T(2,128)(2,1)S(1)} %collective-permute-done.36), channel_id=1, source_target_pairs={{0,128},{128,0},{8,136},{136,8},{16,144},{144,16},{24,152},{152,24... | collective-permute-start | bytes 58376 | tf_op jit(solution)/shard_map/ppermute | solution.py:18
  239.0 19.9 %collective-permute-start.39 = (f32[2,38,1,130]{3,2,1,0:T(1,128)}, f32[2,38,1,130]{3,2,1,0:T(1,128)}, u32[]{:S(2)}, u32[]{:S(2)}) collective-permute-start(f32[2,38,1,130]{3,2,1,0:T(1,128)} %get-tuple-element.109), channel_id=1, source_target_pairs={{0,1},{1,2},{2,3},{3,4},{4,5},{5,6},{6,7},{7,0},{8,9},{9,10},{10,1... | collective-permute-start | bytes 118568 | tf_op jit(solution)/shard_map/ppermute | solution.py:28
  249.0 6.8 %collective-permute-start.38 = (bf16[2,38,128]{2,0,1:T(2,128)(2,1)}, bf16[2,38,128]{2,0,1:T(2,128)(2,1)S(1)}, u32[]{:S(2)}, u32[]{:S(2)}) collective-permute-start(bf16[2,38,128]{2,0,1:T(2,128)(2,1)} %collective-permute-done.37), channel_id=1, source_target_pairs={{0,256},{256,0},{8,264},{264,8},{16,272},{272,16},{24,280},{280,24... | collective-permute-start | bytes 58376 | tf_op jit(solution)/shard_map/ppermute | solution.py:18
  (24 other events, 90.9 us)
where the time goes:
time: 264 us; the launch traced here: 262 us
  starting transfers between devices  167 us (63%)
  waiting for transfers between devices  35.3 us (13%)
  other arithmetic  31.8 us (12%)
  local copies, waits for them, and re-layouts  26 us (10%)
    ppermute x24, starting transfers between devices, from_partner(): return lax.ppermute(block, axis, route)  72.1 us
    ppermute x8, starting transfers between devices, with_halo(): after = lax.ppermute(first, axis, down)  38.9 us
    ppermute x8, starting transfers between devices, with_halo(): before = lax.ppermute(last, axis, up)  36.7 us
    ppermute x24, waiting for transfers between devices, from_partner(): return lax.ppermute(block, axis, route)  20.2 us
    all_to_all x2, starting transfers between devices, shards(): lax.all_to_all(request, 'lat', split_axis=2, concat_axis=2, tiled=True)  19.3 us
    all_to_all x2, waiting for transfers between devices, shards(): lax.all_to_all(request, 'lat', split_axis=2, concat_axis=2, tiled=True)  8.44 us
    unnamed x64, local copies, waits for them, and re-layouts  7.48 us
    ppermute x8, waiting for transfers between devices, with_halo(): after = lax.ppermute(first, axis, down)  6.61 us
  transfers between devices with their start and end apart: 42, of which 10 were waited for; matrix products, arithmetic and copies ran while one was open for 18% of the time, Pallas kernels for 0%

commit v1 on v0

--- a/solution.py
+++ b/solution.py
@@ -111,7 +111,10 @@
     merid_total = jnp.zeros((levels, tile_height, tile_width), jnp.float32)
     for step_index in range(STEPS - 1, -1, -1):
         request = jnp.take(store, slot_table[step_index], axis=2)
-        received = lax.all_to_all(request, "lat", split_axis=2, concat_axis=2, tiled=True)
+        even = lax.all_to_all(
+            jnp.stack(jnp.split(request, lax.axis_size("lat"), axis=2)), "lat", 0, 0
+        )
+        received = jnp.concatenate(even, axis=2)
         order = (jnp.arange(bands, dtype=jnp.int32) + offset_steps[step_index]) % bands
         ordered = jnp.take(received, order, axis=2)
         trajectory = ordered.reshape(received.shape[0], received.shape[1], tile_height, tile_width)

time: 264 us -> 273 us (1.034)
  local copies, waits for them, and re-layouts: 26 us -> 35.9 us
    unnamed x64 -> x78, local copies, waits for them, and re-layouts: 7.48 us -> 16.3 us
  transfers between devices with their start and end apart: 42 -> 42, of which waited for: 10 -> 10; matrix products, arithmetic and copies ran while one was open for 18% -> 19% of each run, Pallas kernels for 0% -> 0%
where the time goes in v1:
time: 273 us; the launch traced here: 271 us
  starting transfers between devices  167 us (61%)
  local copies, waits for them, and re-layouts  35.9 us (13%)
  waiting for transfers between devices  35.8 us (13%)
  other arithmetic  30.8 us (11%)
    ppermute x24, starting transfers between devices, from_partner(): return lax.ppermute(block, axis, route)  71.6 us
    ppermute x8, starting transfers between devices, with_halo(): after = lax.ppermute(first, axis, down)  39 us
    ppermute x8, starting transfers between devices, with_halo(): before = lax.ppermute(last, axis, up)  36.7 us
    ppermute x24, waiting for transfers between devices, from_partner(): return lax.ppermute(block, axis, route)  20.8 us
    all_to_all x2, starting transfers between devices, shards(): lax.all_to_all(jnp.stack(jnp.split(request, lax.axis_size('lat'), axis=2)...  19.4 us
    unnamed x78, local copies, waits for them, and re-layouts  16.3 us
    all_to_all x2, waiting for transfers between devices, shards(): lax.all_to_all(jnp.stack(jnp.split(request, lax.axis_size('lat'), axis=2)...  8.39 us
    ppermute x8, waiting for transfers between devices, with_halo(): after = lax.ppermute(first, axis, down)  6.62 us
  transfers between devices with their start and end apart: 42, of which 10 were waited for; matrix products, arithmetic and copies ran while one was open for 19% of the time, Pallas kernels for 0%

profile of v1, /device:TPU:6, one launch (start us, length us, event | category | flops | bytes accessed | tf_op | source)
XLA Modules:
  0.0 270.9 jit_solution(8069381072226627563)
XLA Ops:
  9.4 10.2 %all-to-all-start.1 = ((bf16[8,4,38,1,1,128]{5,1,2,4,3,0:T(4,128)(2,1)}), bf16[8,4,38,1,1,128]{5,1,2,4,3,0:T(4,128)(2,1)S(1)}, u32[]{:S(2)}, u32[]{:S(2)}) async-start(bf16[8,4,38,1,1,128]{5,1,2,4,3,0:T(4,128)(2,1)} %fusion.54), calls=%async_computation.1 | async-start | bytes 622592 | tf_op jit(solution)/shard_map/all_to_all | solution.py:114
  20.4 10.2 %collective-permute-start = (f32[2,38,8,1]{3,2,1,0:T(8,128)S(1)}, f32[2,38,8,1]{3,2,1,0:T(8,128)S(1)}, u32[]{:S(2)}, u32[]{:S(2)}) collective-permute-start(f32[2,38,8,1]{3,2,1,0:T(8,128)S(1)} %get-tuple-element.132), channel_id=1, source_target_pairs={{8,0},{16,8},{24,16},{32,24},{40,32},{48,40},{56,48},{64,56},{72,6... | collective-permute-start | bytes 7304 | tf_op jit(solution)/shard_map/ppermute | solution.py:29
  30.6 1.9 collective-permute-start.5
  32.6 1.9 collective-permute-start.13
  45.1 5.1 %select_add_fusion = f32[37,8,128]{2,1,0:T(8,128)S(1)} fusion(s32[37,8,128]{2,1,0:T(8,128)S(1)} %copy-done.26, f32[]{:T(128)} %bitcast.38, f32[]{:T(128)} %bitcast.37, f32[]{:T(128)} %bitcast.36, f32[]{:T(128)} %bitcast.35, f32[]{:T(128)} %bitcast.34, f32[]{:T(128)} %bitcast.33, f32[]{:T(128)} %bitcast.32, f32[]{:T(128)} %bitcast.31), kind=kLoop, calls=%fused_computation.94 | loop fusion | flops 871424 | bytes 303136 | tf_op jit(solution)/shard_map/add | solution.py:91
  51.0 1.9 collective-permute-start.14
  53.6 3.1 %collective-permute-done.14 = bf16[2,38,128]{2,0,1:T(2,128)(2,1)S(1)} collective-permute-done((bf16[2,38,128]{2,0,1:T(2,128)(2,1)S(1)}, bf16[2,38,128]{2,0,1:T(2,128)(2,1)S(1)}, u32[]{:S(2)}, u32[]{:S(2)}) %collective-permute-start.14) | collective-permute-done | bytes 19488 | tf_op jit(solution)/shard_map/ppermute | solution.py:18
  59.2 4.0 %collective-permute-done.15 = bf16[2,38,128]{2,0,1:T(2,128)(2,1)S(1)} collective-permute-done((bf16[2,38,128]{2,0,1:T(2,128)(2,1)S(1)}, bf16[2,38,128]{2,0,1:T(2,128)(2,1)S(1)}, u32[]{:S(2)}, u32[]{:S(2)}) %collective-permute-start.15) | collective-permute-done | bytes 19488 | tf_op jit(solution)/shard_map/ppermute | solution.py:18
  63.3 4.7 %collective-permute-start.16 = (bf16[2,38,128]{2,0,1:T(2,128)(2,1)S(1)}, bf16[2,38,128]{2,0,1:T(2,128)(2,1)S(1)}, u32[]{:S(2)}, u32[]{:S(2)}) collective-permute-start(bf16[2,38,128]{2,0,1:T(2,128)(2,1)S(1)} %collective-permute-done.15), channel_id=1, source_target_pairs={{0,64},{64,0},{8,72},{72,8},{16,80},{80,16},{24,88},{88,24},{32,96... | collective-permute-start | bytes 58376 | tf_op jit(solution)/shard_map/ppermute | solution.py:18
  68.5 2.8 %collective-permute-start.12 = (f32[2,38,1,130]{3,2,1,0:T(1,128)S(1)}, f32[2,38,1,130]{3,2,1,0:T(1,128)S(1)}, u32[]{:S(2)}, u32[]{:S(2)}) collective-permute-start(f32[2,38,1,130]{3,2,1,0:T(1,128)S(1)} %get-tuple-element.112), channel_id=1, source_target_pairs={{1,0},{2,1},{3,2},{4,3},{5,4},{6,5},{7,6},{0,7},{9,8},{10,9},{11,1... | collective-permute-start | bytes 118568 | tf_op jit(solution)/shard_map/ppermute | solution.py:29
  72.8 3.0 %collective-permute-start.17 = (bf16[2,38,128]{2,0,1:T(2,128)(2,1)S(1)}, bf16[2,38,128]{2,0,1:T(2,128)(2,1)S(1)}, u32[]{:S(2)}, u32[]{:S(2)}) collective-permute-start(bf16[2,38,128]{2,0,1:T(2,128)(2,1)S(1)} %collective-permute-done.16), channel_id=1, source_target_pairs={{0,128},{128,0},{8,136},{136,8},{16,144},{144,16},{24,152},{152,24... | collective-permute-start | bytes 58376 | tf_op jit(solution)/shard_map/ppermute | solution.py:18
  75.9 7.3 %collective-permute-start.19 = (f32[2,38,1,130]{3,2,1,0:T(1,128)S(1)}, f32[2,38,1,130]{3,2,1,0:T(1,128)}, u32[]{:S(2)}, u32[]{:S(2)}) collective-permute-start(f32[2,38,1,130]{3,2,1,0:T(1,128)S(1)} %get-tuple-element.113), channel_id=1, source_target_pairs={{0,1},{1,2},{2,3},{3,4},{4,5},{5,6},{6,7},{7,0},{8,9},{9,10},{10,1... | collective-permute-start | bytes 118568 | tf_op jit(solution)/shard_map/ppermute | solution.py:28
  83.2 4.4 %collective-permute-start.18 = (bf16[2,38,128]{2,0,1:T(2,128)(2,1)S(1)}, bf16[2,38,128]{2,0,1:T(2,128)(2,1)S(1)}, u32[]{:S(2)}, u32[]{:S(2)}) collective-permute-start(bf16[2,38,128]{2,0,1:T(2,128)(2,1)S(1)} %collective-permute-done.17), channel_id=1, source_target_pairs={{0,256},{256,0},{8,264},{264,8},{16,272},{272,16},{24,280},{280,24... | collective-permute-start | bytes 58376 | tf_op jit(solution)/shard_map/ppermute | solution.py:18
  90.9 9.2 %all-to-all-start = ((bf16[8,4,38,1,1,128]{5,1,2,4,3,0:T(4,128)(2,1)}), bf16[8,4,38,1,1,128]{5,1,2,4,3,0:T(4,128)(2,1)S(1)}, u32[]{:S(2)}, u32[]{:S(2)}) async-start(bf16[8,4,38,1,1,128]{5,1,2,4,3,0:T(4,128)(2,1)} %fusion.62), calls=%async_computation | async-start | bytes 622592 | tf_op jit(solution)/shard_map/all_to_all | solution.py:114
  102.1 8.4 %all-to-all-done = bf16[8,4,38,1,1,128]{5,1,2,4,3,0:T(4,128)(2,1)S(1)} async-done(((bf16[8,4,38,1,1,128]{5,1,2,4,3,0:T(4,128)(2,1)}), bf16[8,4,38,1,1,128]{5,1,2,4,3,0:T(4,128)(2,1)S(1)}, u32[]{:S(2)}, u32[]{:S(2)}) %all-to-all-start) | async-done | bytes 311328 | tf_op jit(solution)/shard_map/all_to_all | solution.py:114
  114.0 7.5 %collective-permute-start.22 = (bf16[4,38,8,1]{3,2,1,0:T(8,128)(2,1)S(1)}, bf16[4,38,8,1]{3,2,1,0:T(8,128)(2,1)S(1)}, u32[]{:S(2)}, u32[]{:S(2)}) collective-permute-start(bf16[4,38,8,1]{3,2,1,0:T(8,128)(2,1)S(1)} %get-tuple-element.120), channel_id=1, source_target_pairs={{8,0},{16,8},{24,16},{32,24},{40,32},{48,40},{56,48},{64,56},{72,6... | collective-permute-start | bytes 7304 | tf_op jit(solution)/shard_map/ppermute | solution.py:29
  121.5 1.9 collective-permute-start.1
  123.5 7.5 %collective-permute-start.2 = (bf16[4,38,8,1]{3,2,1,0:T(8,128)(2,1)S(1)}, bf16[4,38,8,1]{3,2,1,0:T(8,128)(2,1)S(1)}, u32[]{:S(2)}, u32[]{:S(2)}) collective-permute-start(bf16[4,38,8,1]{3,2,1,0:T(8,128)(2,1)S(1)} %get-tuple-element.131), channel_id=1, source_target_pairs={{8,0},{16,8},{24,16},{32,24},{40,32},{48,40},{56,48},{64,56},{72,6... | collective-permute-start | bytes 7304 | tf_op jit(solution)/shard_map/ppermute | solution.py:29
  132.6 1.9 collective-permute-start.26
  134.6 2.4 collective-permute-start.6
  137.8 2.9 %collective-permute-start.23 = (bf16[4,38,1,130]{3,2,1,0:T(2,128)(2,1)S(1)}, bf16[4,38,1,130]{3,2,1,0:T(2,128)(2,1)S(1)}, u32[]{:S(2)}, u32[]{:S(2)}) collective-permute-start(bf16[4,38,1,130]{3,2,1,0:T(2,128)(2,1)S(1)} %get-tuple-element.106), channel_id=1, source_target_pairs={{0,1},{1,2},{2,3},{3,4},{4,5},{5,6},{6,7},{7,0},{8,9},{9,10},{10,1... | collective-permute-start | bytes 118568 | tf_op jit(solution)/shard_map/ppermute | solution.py:28
  140.7 2.9 %collective-permute-start.24 = (bf16[4,38,1,130]{3,2,1,0:T(2,128)(2,1)S(1)}, bf16[4,38,1,130]{3,2,1,0:T(2,128)(2,1)S(1)}, u32[]{:S(2)}, u32[]{:S(2)}) collective-permute-start(bf16[4,38,1,130]{3,2,1,0:T(2,128)(2,1)S(1)} %get-tuple-element.107), channel_id=1, source_target_pairs={{1,0},{2,1},{3,2},{4,3},{5,4},{6,5},{7,6},{0,7},{9,8},{10,9},{11,1... | collective-permute-start | bytes 118568 | tf_op jit(solution)/shard_map/ppermute | solution.py:29
  144.4 8.9 %collective-permute-start.3 = (bf16[4,38,1,130]{3,2,1,0:T(2,128)(2,1)S(1)}, bf16[4,38,1,130]{3,2,1,0:T(2,128)(2,1)S(1)}, u32[]{:S(2)}, u32[]{:S(2)}) collective-permute-start(bf16[4,38,1,130]{3,2,1,0:T(2,128)(2,1)S(1)} %get-tuple-element.110), channel_id=1, source_target_pairs={{0,1},{1,2},{2,3},{3,4},{4,5},{5,6},{6,7},{7,0},{8,9},{9,10},{10,1... | collective-permute-start | bytes 118568 | tf_op jit(solution)/shard_map/ppermute | solution.py:28
  153.4 1.9 collective-permute-start.4
  155.3 1.9 collective-permute-start.27
  157.3 3.9 %collective-permute-start.7 = (bf16[3,38,128]{2,0,1:T(4,128)(2,1)S(1)}, bf16[3,38,128]{2,0,1:T(4,128)(2,1)S(1)}, u32[]{:S(2)}, u32[]{:S(2)}) collective-permute-start(bf16[3,38,128]{2,0,1:T(4,128)(2,1)S(1)} %collective-permute-done.6), channel_id=1, source_target_pairs={{0,16},{16,0},{8,24},{24,8},{32,48},{48,32},{40,56},{56,40},{64,80... | collective-permute-start | bytes 87560 | tf_op jit(solution)/shard_map/ppermute | solution.py:18
  162.3 6.6 %collective-permute-done.4 = bf16[4,38,1,130]{3,2,1,0:T(2,128)(2,1)S(1)} collective-permute-done((bf16[4,38,1,130]{3,2,1,0:T(2,128)(2,1)S(1)}, bf16[4,38,1,130]{3,2,1,0:T(2,128)(2,1)S(1)}, u32[]{:S(2)}, u32[]{:S(2)}) %collective-permute-start.4) | collective-permute-done | bytes 39552 | tf_op jit(solution)/shard_map/ppermute | solution.py:29
  173.6 4.8 %collective-permute-start.28 = (bf16[3,38,128]{2,0,1:T(4,128)(2,1)S(1)}, bf16[3,38,128]{2,0,1:T(4,128)(2,1)S(1)}, u32[]{:S(2)}, u32[]{:S(2)}) collective-permute-start(bf16[3,38,128]{2,0,1:T(4,128)(2,1)S(1)} %collective-permute-done.27), channel_id=1, source_target_pairs={{0,32},{32,0},{8,40},{40,8},{16,48},{48,16},{24,56},{56,24},{64,96... | collective-permute-start | bytes 87560 | tf_op jit(solution)/shard_map/ppermute | solution.py:18
  178.4 1.9 collective-permute-start.9
  181.1 7.8 %collective-permute-start.29 = (bf16[3,38,128]{2,0,1:T(4,128)(2,1)S(1)}, bf16[3,38,128]{2,0,1:T(4,128)(2,1)S(1)}, u32[]{:S(2)}, u32[]{:S(2)}) collective-permute-start(bf16[3,38,128]{2,0,1:T(4,128)(2,1)S(1)} %collective-permute-done.28), channel_id=1, source_target_pairs={{0,64},{64,0},{8,72},{72,8},{16,80},{80,16},{24,88},{88,24},{32,96... | collective-permute-start | bytes 87560 | tf_op jit(solution)/shard_map/ppermute | solution.py:18
  191.1 3.9 %collective-permute-start.30 = (bf16[3,38,128]{2,0,1:T(4,128)(2,1)S(1)}, bf16[3,38,128]{2,0,1:T(4,128)(2,1)}, u32[]{:S(2)}, u32[]{:S(2)}) collective-permute-start(bf16[3,38,128]{2,0,1:T(4,128)(2,1)S(1)} %collective-permute-done.29), channel_id=1, source_target_pairs={{0,128},{128,0},{8,136},{136,8},{16,144},{144,16},{24,152},{152,24... | collective-permute-start | bytes 87560 | tf_op jit(solution)/shard_map/ppermute | solution.py:18
  195.0 2.1 collective-permute-start.11
  197.9 4.8 %collective-permute-start.31 = (bf16[3,38,128]{2,0,1:T(4,128)(2,1)}, bf16[3,38,128]{2,0,1:T(4,128)(2,1)}, u32[]{:S(2)}, u32[]{:S(2)}) collective-permute-start(bf16[3,38,128]{2,0,1:T(4,128)(2,1)} %collective-permute-done.30), channel_id=1, source_target_pairs={{0,256},{256,0},{8,264},{264,8},{16,272},{272,16},{24,280},{280,24... | collective-permute-start | bytes 87560 | tf_op jit(solution)/shard_map/ppermute | solution.py:18
  203.7 2.0 fusion.31
  211.1 4.0 %collective-permute-start.20 = (f32[2,38,8,1]{3,2,1,0:T(8,128)}, f32[2,38,8,1]{3,2,1,0:T(8,128)S(1)}, u32[]{:S(2)}, u32[]{:S(2)}) collective-permute-start(f32[2,38,8,1]{3,2,1,0:T(8,128)} %get-tuple-element.121), channel_id=1, source_target_pairs={{8,0},{16,8},{24,16},{32,24},{40,32},{48,40},{56,48},{64,56},{72,6... | collective-permute-start | bytes 7304 | tf_op jit(solution)/shard_map/ppermute | solution.py:29
  215.1 1.9 collective-permute-start.25
  217.1 1.9 collective-permute-start.34
  219.7 3.4 %collective-permute-done.34 = bf16[2,38,128]{2,0,1:T(2,128)(2,1)} collective-permute-done((bf16[2,38,128]{2,0,1:T(2,128)(2,1)}, bf16[2,38,128]{2,0,1:T(2,128)(2,1)}, u32[]{:S(2)}, u32[]{:S(2)}) %collective-permute-start.34) | collective-permute-done | bytes 19488 | tf_op jit(solution)/shard_map/ppermute | solution.py:18
  227.8 2.1 collective-permute-done.35
  229.9 4.2 %collective-permute-start.36 = (bf16[2,38,128]{2,0,1:T(2,128)(2,1)}, bf16[2,38,128]{2,0,1:T(2,128)(2,1)S(1)}, u32[]{:S(2)}, u32[]{:S(2)}) collective-permute-start(bf16[2,38,128]{2,0,1:T(2,128)(2,1)} %collective-permute-done.35), channel_id=1, source_target_pairs={{0,64},{64,0},{8,72},{72,8},{16,80},{80,16},{24,88},{88,24},{32,96... | collective-permute-start | bytes 58376 | tf_op jit(solution)/shard_map/ppermute | solution.py:18
  234.2 2.3 pad_maximum_fusion.25
  236.4 2.0 collective-permute-start.32
  239.9 2.5 collective-permute-start.37
  242.5 2.2 fusion.1
  248.1 9.9 %collective-permute-start.39 = (f32[2,38,1,130]{3,2,1,0:T(1,128)}, f32[2,38,1,130]{3,2,1,0:T(1,128)}, u32[]{:S(2)}, u32[]{:S(2)}) collective-permute-start(f32[2,38,1,130]{3,2,1,0:T(1,128)} %get-tuple-element.109), channel_id=1, source_target_pairs={{0,1},{1,2},{2,3},{3,4},{4,5},{5,6},{6,7},{7,0},{8,9},{9,10},{10,1... | collective-permute-start | bytes 118568 | tf_op jit(solution)/shard_map/ppermute | solution.py:28
  258.0 2.0 collective-permute-start.38
  261.5 3.4 %collective-permute-done.38 = bf16[2,38,128]{2,0,1:T(2,128)(2,1)S(1)} collective-permute-done((bf16[2,38,128]{2,0,1:T(2,128)(2,1)}, bf16[2,38,128]{2,0,1:T(2,128)(2,1)S(1)}, u32[]{:S(2)}, u32[]{:S(2)}) %collective-permute-start.38) | collective-permute-done | bytes 19488 | tf_op jit(solution)/shard_map/ppermute | solution.py:18
  268.6 2.3 fusion.15
  (207 shorter events, 69.1 us)
Async XLA Ops:
  9.4 80.8 %all-to-all-start.1 = ((bf16[8,4,38,1,1,128]{5,1,2,4,3,0:T(4,128)(2,1)}), bf16[8,4,38,1,1,128]{5,1,2,4,3,0:T(4,128)(2,1)S(1)}, u32[]{:S(2)}, u32[]{:S(2)}) async-start(bf16[8,4,38,1,1,128]{5,1,2,4,3,0:T(4,128)(2,1)} %fusion.54), calls=%async_computation.1 | async-start | bytes 622592 | tf_op jit(solution)/shard_map/all_to_all | solution.py:114
  20.4 47.5 %collective-permute-start = (f32[2,38,8,1]{3,2,1,0:T(8,128)S(1)}, f32[2,38,8,1]{3,2,1,0:T(8,128)S(1)}, u32[]{:S(2)}, u32[]{:S(2)}) collective-permute-start(f32[2,38,8,1]{3,2,1,0:T(8,128)S(1)} %get-tuple-element.132), channel_id=1, source_target_pairs={{8,0},{16,8},{24,16},{32,24},{40,32},{48,40},{56,48},{64,56},{72,6... | collective-permute-start | bytes 7304 | tf_op jit(solution)/shard_map/ppermute | solution.py:29
  30.6 37.4 %collective-permute-start.5 = (f32[2,38,8,1]{3,2,1,0:T(8,128)S(1)}, f32[2,38,8,1]{3,2,1,0:T(8,128)S(1)}, u32[]{:S(2)}, u32[]{:S(2)}) collective-permute-start(f32[2,38,8,1]{3,2,1,0:T(8,128)S(1)} %get-tuple-element.133), channel_id=1, source_target_pairs={{0,8},{8,16},{16,24},{24,32},{32,40},{40,48},{48,56},{56,64},{64,7... | collective-permute-start | bytes 7304 | tf_op jit(solution)/shard_map/ppermute | solution.py:28
  32.6 18.4 %collective-permute-start.13 = (bf16[2,38,128]{2,0,1:T(2,128)(2,1)S(1)}, bf16[2,38,128]{2,0,1:T(2,128)(2,1)S(1)}, u32[]{:S(2)}, u32[]{:S(2)}) collective-permute-start(bf16[2,38,128]{2,0,1:T(2,128)(2,1)S(1)} %bitcast.215), channel_id=1, source_target_pairs={{0,8},{8,0},{16,24},{24,16},{32,40},{40,32},{48,56},{56,48},{64,72... | collective-permute-start | bytes 58376 | tf_op jit(solution)/shard_map/ppermute | solution.py:18
  51.0 5.7 %collective-permute-start.14 = (bf16[2,38,128]{2,0,1:T(2,128)(2,1)S(1)}, bf16[2,38,128]{2,0,1:T(2,128)(2,1)S(1)}, u32[]{:S(2)}, u32[]{:S(2)}) collective-permute-start(bf16[2,38,128]{2,0,1:T(2,128)(2,1)S(1)} %collective-permute-done.13), channel_id=1, source_target_pairs={{0,16},{16,0},{8,24},{24,8},{32,48},{48,32},{40,56},{56,40},{64,80... | collective-permute-start | bytes 58376 | tf_op jit(solution)/shard_map/ppermute | solution.py:18
  56.7 6.6 %collective-permute-start.15 = (bf16[2,38,128]{2,0,1:T(2,128)(2,1)S(1)}, bf16[2,38,128]{2,0,1:T(2,128)(2,1)S(1)}, u32[]{:S(2)}, u32[]{:S(2)}) collective-permute-start(bf16[2,38,128]{2,0,1:T(2,128)(2,1)S(1)} %collective-permute-done.14), channel_id=1, source_target_pairs={{0,32},{32,0},{8,40},{40,8},{16,48},{48,16},{24,56},{56,24},{64,96... | collective-permute-start | bytes 58376 | tf_op jit(solution)/shard_map/ppermute | solution.py:18
  63.3 9.6 %collective-permute-start.16 = (bf16[2,38,128]{2,0,1:T(2,128)(2,1)S(1)}, bf16[2,38,128]{2,0,1:T(2,128)(2,1)S(1)}, u32[]{:S(2)}, u32[]{:S(2)}) collective-permute-start(bf16[2,38,128]{2,0,1:T(2,128)(2,1)S(1)} %collective-permute-done.15), channel_id=1, source_target_pairs={{0,64},{64,0},{8,72},{72,8},{16,80},{80,16},{24,88},{88,24},{32,96... | collective-permute-start | bytes 58376 | tf_op jit(solution)/shard_map/ppermute | solution.py:18
  68.5 19.0 %collective-permute-start.12 = (f32[2,38,1,130]{3,2,1,0:T(1,128)S(1)}, f32[2,38,1,130]{3,2,1,0:T(1,128)S(1)}, u32[]{:S(2)}, u32[]{:S(2)}) collective-permute-start(f32[2,38,1,130]{3,2,1,0:T(1,128)S(1)} %get-tuple-element.112), channel_id=1, source_target_pairs={{1,0},{2,1},{3,2},{4,3},{5,4},{6,5},{7,6},{0,7},{9,8},{10,9},{11,1... | collective-permute-start | bytes 118568 | tf_op jit(solution)/shard_map/ppermute | solution.py:29
  72.8 10.3 %collective-permute-start.17 = (bf16[2,38,128]{2,0,1:T(2,128)(2,1)S(1)}, bf16[2,38,128]{2,0,1:T(2,128)(2,1)S(1)}, u32[]{:S(2)}, u32[]{:S(2)}) collective-permute-start(bf16[2,38,128]{2,0,1:T(2,128)(2,1)S(1)} %collective-permute-done.16), channel_id=1, source_target_pairs={{0,128},{128,0},{8,136},{136,8},{16,144},{144,16},{24,152},{152,24... | collective-permute-start | bytes 58376 | tf_op jit(solution)/shard_map/ppermute | solution.py:18
  75.9 127.2 %collective-permute-start.19 = (f32[2,38,1,130]{3,2,1,0:T(1,128)S(1)}, f32[2,38,1,130]{3,2,1,0:T(1,128)}, u32[]{:S(2)}, u32[]{:S(2)}) collective-permute-start(f32[2,38,1,130]{3,2,1,0:T(1,128)S(1)} %get-tuple-element.113), channel_id=1, source_target_pairs={{0,1},{1,2},{2,3},{3,4},{4,5},{5,6},{6,7},{7,0},{8,9},{9,10},{10,1... | collective-permute-start | bytes 118568 | tf_op jit(solution)/shard_map/ppermute | solution.py:28
  83.2 6.6 %collective-permute-start.18 = (bf16[2,38,128]{2,0,1:T(2,128)(2,1)S(1)}, bf16[2,38,128]{2,0,1:T(2,128)(2,1)S(1)}, u32[]{:S(2)}, u32[]{:S(2)}) collective-permute-start(bf16[2,38,128]{2,0,1:T(2,128)(2,1)S(1)} %collective-permute-done.17), channel_id=1, source_target_pairs={{0,256},{256,0},{8,264},{264,8},{16,272},{272,16},{24,280},{280,24... | collective-permute-start | bytes 58376 | tf_op jit(solution)/shard_map/ppermute | solution.py:18
  90.9 19.6 %all-to-all-start = ((bf16[8,4,38,1,1,128]{5,1,2,4,3,0:T(4,128)(2,1)}), bf16[8,4,38,1,1,128]{5,1,2,4,3,0:T(4,128)(2,1)S(1)}, u32[]{:S(2)}, u32[]{:S(2)}) async-start(bf16[8,4,38,1,1,128]{5,1,2,4,3,0:T(4,128)(2,1)} %fusion.62), calls=%async_computation | async-start | bytes 622592 | tf_op jit(solution)/shard_map/all_to_all | solution.py:114
  111.9 19.1 %copy-start.11 = (bf16[4,38,8,1,128]{4,2,1,3,0:T(8,128)(2,1)}, bf16[4,38,8,1,128]{4,2,1,3,0:T(8,128)(2,1)S(1)}, u32[]{:S(2)}) copy-start(bf16[4,38,8,1,128]{4,2,1,3,0:T(8,128)(2,1)S(1)} %bitcast_select_fusion.2) | copy-start | bytes 933892
  112.1 20.4 %copy-start.9 = (bf16[4,38,8,1,128]{4,2,1,0,3:T(8,128)(2,1)}, bf16[4,38,8,1,128]{4,2,1,0,3:T(8,128)(2,1)S(1)}, u32[]{:S(2)}) copy-start(bf16[4,38,8,1,128]{4,2,1,0,3:T(8,128)(2,1)S(1)} %bitcast_select_fusion) | copy-start | bytes 933892
  112.1 20.6 %collective-permute-start.21 = (bf16[4,38,8,1]{3,2,1,0:T(8,128)(2,1)}, bf16[4,38,8,1]{3,2,1,0:T(8,128)(2,1)S(1)}, u32[]{:S(2)}, u32[]{:S(2)}) collective-permute-start(bf16[4,38,8,1]{3,2,1,0:T(8,128)(2,1)} %get-tuple-element.119), channel_id=1, source_target_pairs={{0,8},{8,16},{16,24},{24,32},{32,40},{40,48},{48,56},{56,64},{64,7... | collective-permute-start | bytes 7304 | tf_op jit(solution)/shard_map/ppermute | solution.py:28
  114.0 20.6 %collective-permute-start.22 = (bf16[4,38,8,1]{3,2,1,0:T(8,128)(2,1)S(1)}, bf16[4,38,8,1]{3,2,1,0:T(8,128)(2,1)S(1)}, u32[]{:S(2)}, u32[]{:S(2)}) collective-permute-start(bf16[4,38,8,1]{3,2,1,0:T(8,128)(2,1)S(1)} %get-tuple-element.120), channel_id=1, source_target_pairs={{8,0},{16,8},{24,16},{32,24},{40,32},{48,40},{56,48},{64,56},{72,6... | collective-permute-start | bytes 7304 | tf_op jit(solution)/shard_map/ppermute | solution.py:29
  121.5 16.2 %collective-permute-start.1 = (bf16[4,38,8,1]{3,2,1,0:T(8,128)(2,1)S(1)}, bf16[4,38,8,1]{3,2,1,0:T(8,128)(2,1)S(1)}, u32[]{:S(2)}, u32[]{:S(2)}) collective-permute-start(bf16[4,38,8,1]{3,2,1,0:T(8,128)(2,1)S(1)} %get-tuple-element.130), channel_id=1, source_target_pairs={{0,8},{8,16},{16,24},{24,32},{32,40},{40,48},{48,56},{56,64},{64,7... | collective-permute-start | bytes 7304 | tf_op jit(solution)/shard_map/ppermute | solution.py:28
  123.5 17.2 %collective-permute-start.2 = (bf16[4,38,8,1]{3,2,1,0:T(8,128)(2,1)S(1)}, bf16[4,38,8,1]{3,2,1,0:T(8,128)(2,1)S(1)}, u32[]{:S(2)}, u32[]{:S(2)}) collective-permute-start(bf16[4,38,8,1]{3,2,1,0:T(8,128)(2,1)S(1)} %get-tuple-element.131), channel_id=1, source_target_pairs={{8,0},{16,8},{24,16},{32,24},{40,32},{48,40},{56,48},{64,56},{72,6... | collective-permute-start | bytes 7304 | tf_op jit(solution)/shard_map/ppermute | solution.py:29
  132.6 11.8 %collective-permute-start.26 = (bf16[3,38,128]{2,0,1:T(4,128)(2,1)S(1)}, bf16[3,38,128]{2,0,1:T(4,128)(2,1)S(1)}, u32[]{:S(2)}, u32[]{:S(2)}) collective-permute-start(bf16[3,38,128]{2,0,1:T(4,128)(2,1)S(1)} %pad_maximum_fusion.38), channel_id=1, source_target_pairs={{0,8},{8,0},{16,24},{24,16},{32,40},{40,32},{48,56},{56,48},{64,72... | collective-permute-start | bytes 87560 | tf_op jit(solution)/shard_map/ppermute | solution.py:18
  134.6 18.8 %collective-permute-start.6 = (bf16[3,38,128]{2,0,1:T(4,128)(2,1)S(1)}, bf16[3,38,128]{2,0,1:T(4,128)(2,1)S(1)}, u32[]{:S(2)}, u32[]{:S(2)}) collective-permute-start(bf16[3,38,128]{2,0,1:T(4,128)(2,1)S(1)} %pad_maximum_fusion.37), channel_id=1, source_target_pairs={{0,8},{8,0},{16,24},{24,16},{32,40},{40,32},{48,56},{56,48},{64,72... | collective-permute-start | bytes 87560 | tf_op jit(solution)/shard_map/ppermute | solution.py:18
  137.8 17.5 %collective-permute-start.23 = (bf16[4,38,1,130]{3,2,1,0:T(2,128)(2,1)S(1)}, bf16[4,38,1,130]{3,2,1,0:T(2,128)(2,1)S(1)}, u32[]{:S(2)}, u32[]{:S(2)}) collective-permute-start(bf16[4,38,1,130]{3,2,1,0:T(2,128)(2,1)S(1)} %get-tuple-element.106), channel_id=1, source_target_pairs={{0,1},{1,2},{2,3},{3,4},{4,5},{5,6},{6,7},{7,0},{8,9},{9,10},{10,1... | collective-permute-start | bytes 118568 | tf_op jit(solution)/shard_map/ppermute | solution.py:28
  140.7 16.5 %collective-permute-start.24 = (bf16[4,38,1,130]{3,2,1,0:T(2,128)(2,1)S(1)}, bf16[4,38,1,130]{3,2,1,0:T(2,128)(2,1)S(1)}, u32[]{:S(2)}, u32[]{:S(2)}) collective-permute-start(bf16[4,38,1,130]{3,2,1,0:T(2,128)(2,1)S(1)} %get-tuple-element.107), channel_id=1, source_target_pairs={{1,0},{2,1},{3,2},{4,3},{5,4},{6,5},{7,6},{0,7},{9,8},{10,9},{11,1... | collective-permute-start | bytes 118568 | tf_op jit(solution)/shard_map/ppermute | solution.py:29
  144.4 17.9 %collective-permute-start.3 = (bf16[4,38,1,130]{3,2,1,0:T(2,128)(2,1)S(1)}, bf16[4,38,1,130]{3,2,1,0:T(2,128)(2,1)S(1)}, u32[]{:S(2)}, u32[]{:S(2)}) collective-permute-start(bf16[4,38,1,130]{3,2,1,0:T(2,128)(2,1)S(1)} %get-tuple-element.110), channel_id=1, source_target_pairs={{0,1},{1,2},{2,3},{3,4},{4,5},{5,6},{6,7},{7,0},{8,9},{9,10},{10,1... | collective-permute-start | bytes 118568 | tf_op jit(solution)/shard_map/ppermute | solution.py:28
  153.4 15.5 %collective-permute-start.4 = (bf16[4,38,1,130]{3,2,1,0:T(2,128)(2,1)S(1)}, bf16[4,38,1,130]{3,2,1,0:T(2,128)(2,1)S(1)}, u32[]{:S(2)}, u32[]{:S(2)}) collective-permute-start(bf16[4,38,1,130]{3,2,1,0:T(2,128)(2,1)S(1)} %get-tuple-element.111), channel_id=1, source_target_pairs={{1,0},{2,1},{3,2},{4,3},{5,4},{6,5},{7,6},{0,7},{9,8},{10,9},{11,1... | collective-permute-start | bytes 118568 | tf_op jit(solution)/shard_map/ppermute | solution.py:29
  155.3 18.3 %collective-permute-start.27 = (bf16[3,38,128]{2,0,1:T(4,128)(2,1)S(1)}, bf16[3,38,128]{2,0,1:T(4,128)(2,1)S(1)}, u32[]{:S(2)}, u32[]{:S(2)}) collective-permute-start(bf16[3,38,128]{2,0,1:T(4,128)(2,1)S(1)} %collective-permute-done.26), channel_id=1, source_target_pairs={{0,16},{16,0},{8,24},{24,8},{32,48},{48,32},{40,56},{56,40},{64,80... | collective-permute-start | bytes 87560 | tf_op jit(solution)/shard_map/ppermute | solution.py:18
  157.3 13.7 %collective-permute-start.7 = (bf16[3,38,128]{2,0,1:T(4,128)(2,1)S(1)}, bf16[3,38,128]{2,0,1:T(4,128)(2,1)S(1)}, u32[]{:S(2)}, u32[]{:S(2)}) collective-permute-start(bf16[3,38,128]{2,0,1:T(4,128)(2,1)S(1)} %collective-permute-done.6), channel_id=1, source_target_pairs={{0,16},{16,0},{8,24},{24,8},{32,48},{48,32},{40,56},{56,40},{64,80... | collective-permute-start | bytes 87560 | tf_op jit(solution)/shard_map/ppermute | solution.py:18
  162.3 28.6 %copy-start = (bf16[4,38,1,130]{3,2,1,0:T(2,128)(2,1)}, bf16[4,38,1,130]{3,2,1,0:T(2,128)(2,1)S(1)}, u32[]{:S(2)}) copy-start(bf16[4,38,1,130]{3,2,1,0:T(2,128)(2,1)S(1)} %collective-permute-done.3) | copy-start | bytes 118564
  168.9 22.0 %copy-start.2 = (bf16[4,38,1,130]{3,2,1,0:T(2,128)(2,1)}, bf16[4,38,1,130]{3,2,1,0:T(2,128)(2,1)S(1)}, u32[]{:S(2)}) copy-start(bf16[4,38,1,130]{3,2,1,0:T(2,128)(2,1)S(1)} %collective-permute-done.4) | copy-start | bytes 118564
  170.9 7.5 %collective-permute-start.8 = (bf16[3,38,128]{2,0,1:T(4,128)(2,1)S(1)}, bf16[3,38,128]{2,0,1:T(4,128)(2,1)S(1)}, u32[]{:S(2)}, u32[]{:S(2)}) collective-permute-start(bf16[3,38,128]{2,0,1:T(4,128)(2,1)S(1)} %collective-permute-done.7), channel_id=1, source_target_pairs={{0,32},{32,0},{8,40},{40,8},{16,48},{48,16},{24,56},{56,24},{64,96... | collective-permute-start | bytes 87560 | tf_op jit(solution)/shard_map/ppermute | solution.py:18
  173.6 7.5 %collective-permute-start.28 = (bf16[3,38,128]{2,0,1:T(4,128)(2,1)S(1)}, bf16[3,38,128]{2,0,1:T(4,128)(2,1)S(1)}, u32[]{:S(2)}, u32[]{:S(2)}) collective-permute-start(bf16[3,38,128]{2,0,1:T(4,128)(2,1)S(1)} %collective-permute-done.27), channel_id=1, source_target_pairs={{0,32},{32,0},{8,40},{40,8},{16,48},{48,16},{24,56},{56,24},{64,96... | collective-permute-start | bytes 87560 | tf_op jit(solution)/shard_map/ppermute | solution.py:18
  178.4 10.5 %collective-permute-start.9 = (bf16[3,38,128]{2,0,1:T(4,128)(2,1)S(1)}, bf16[3,38,128]{2,0,1:T(4,128)(2,1)S(1)}, u32[]{:S(2)}, u32[]{:S(2)}) collective-permute-start(bf16[3,38,128]{2,0,1:T(4,128)(2,1)S(1)} %collective-permute-done.8), channel_id=1, source_target_pairs={{0,64},{64,0},{8,72},{72,8},{16,80},{80,16},{24,88},{88,24},{32,96... | collective-permute-start | bytes 87560 | tf_op jit(solution)/shard_map/ppermute | solution.py:18
  181.1 9.9 %collective-permute-start.29 = (bf16[3,38,128]{2,0,1:T(4,128)(2,1)S(1)}, bf16[3,38,128]{2,0,1:T(4,128)(2,1)S(1)}, u32[]{:S(2)}, u32[]{:S(2)}) collective-permute-start(bf16[3,38,128]{2,0,1:T(4,128)(2,1)S(1)} %collective-permute-done.28), channel_id=1, source_target_pairs={{0,64},{64,0},{8,72},{72,8},{16,80},{80,16},{24,88},{88,24},{32,96... | collective-permute-start | bytes 87560 | tf_op jit(solution)/shard_map/ppermute | solution.py:18
  189.0 6.0 %collective-permute-start.10 = (bf16[3,38,128]{2,0,1:T(4,128)(2,1)S(1)}, bf16[3,38,128]{2,0,1:T(4,128)(2,1)S(1)}, u32[]{:S(2)}, u32[]{:S(2)}) collective-permute-start(bf16[3,38,128]{2,0,1:T(4,128)(2,1)S(1)} %collective-permute-done.9), channel_id=1, source_target_pairs={{0,128},{128,0},{8,136},{136,8},{16,144},{144,16},{24,152},{152,24... | collective-permute-start | bytes 87560 | tf_op jit(solution)/shard_map/ppermute | solution.py:18
  191.1 6.9 %collective-permute-start.30 = (bf16[3,38,128]{2,0,1:T(4,128)(2,1)S(1)}, bf16[3,38,128]{2,0,1:T(4,128)(2,1)}, u32[]{:S(2)}, u32[]{:S(2)}) collective-permute-start(bf16[3,38,128]{2,0,1:T(4,128)(2,1)S(1)} %collective-permute-done.29), channel_id=1, source_target_pairs={{0,128},{128,0},{8,136},{136,8},{16,144},{144,16},{24,152},{152,24... | collective-permute-start | bytes 87560 | tf_op jit(solution)/shard_map/ppermute | solution.py:18
  195.0 7.7 %collective-permute-start.11 = (bf16[3,38,128]{2,0,1:T(4,128)(2,1)S(1)}, bf16[3,38,128]{2,0,1:T(4,128)(2,1)S(1)}, u32[]{:S(2)}, u32[]{:S(2)}) collective-permute-start(bf16[3,38,128]{2,0,1:T(4,128)(2,1)S(1)} %collective-permute-done.10), channel_id=1, source_target_pairs={{0,256},{256,0},{8,264},{264,8},{16,272},{272,16},{24,280},{280,24... | collective-permute-start | bytes 87560 | tf_op jit(solution)/shard_map/ppermute | solution.py:18
  197.9 12.2 %collective-permute-start.31 = (bf16[3,38,128]{2,0,1:T(4,128)(2,1)}, bf16[3,38,128]{2,0,1:T(4,128)(2,1)}, u32[]{:S(2)}, u32[]{:S(2)}) collective-permute-start(bf16[3,38,128]{2,0,1:T(4,128)(2,1)} %collective-permute-done.30), channel_id=1, source_target_pairs={{0,256},{256,0},{8,264},{264,8},{16,272},{272,16},{24,280},{280,24... | collective-permute-start | bytes 87560 | tf_op jit(solution)/shard_map/ppermute | solution.py:18
  207.4 9.7 %collective-permute-start.33 = (bf16[2,38,128]{2,0,1:T(2,128)(2,1)}, bf16[2,38,128]{2,0,1:T(2,128)(2,1)}, u32[]{:S(2)}, u32[]{:S(2)}) collective-permute-start(bf16[2,38,128]{2,0,1:T(2,128)(2,1)} %bitcast.210), channel_id=1, source_target_pairs={{0,8},{8,0},{16,24},{24,16},{32,40},{40,32},{48,56},{56,48},{64,72... | collective-permute-start | bytes 58376 | tf_op jit(solution)/shard_map/ppermute | solution.py:18
  211.1 23.0 %collective-permute-start.20 = (f32[2,38,8,1]{3,2,1,0:T(8,128)}, f32[2,38,8,1]{3,2,1,0:T(8,128)S(1)}, u32[]{:S(2)}, u32[]{:S(2)}) collective-permute-start(f32[2,38,8,1]{3,2,1,0:T(8,128)} %get-tuple-element.121), channel_id=1, source_target_pairs={{8,0},{16,8},{24,16},{32,24},{40,32},{48,40},{56,48},{64,56},{72,6... | collective-permute-start | bytes 7304 | tf_op jit(solution)/shard_map/ppermute | solution.py:29
  215.1 19.0 %collective-permute-start.25 = (f32[2,38,8,1]{3,2,1,0:T(8,128)}, f32[2,38,8,1]{3,2,1,0:T(8,128)}, u32[]{:S(2)}, u32[]{:S(2)}) collective-permute-start(f32[2,38,8,1]{3,2,1,0:T(8,128)} %get-tuple-element.122), channel_id=1, source_target_pairs={{0,8},{8,16},{16,24},{24,32},{32,40},{40,48},{48,56},{56,64},{64,7... | collective-permute-start | bytes 7304 | tf_op jit(solution)/shard_map/ppermute | solution.py:28
  217.1 6.0 %collective-permute-start.34 = (bf16[2,38,128]{2,0,1:T(2,128)(2,1)}, bf16[2,38,128]{2,0,1:T(2,128)(2,1)}, u32[]{:S(2)}, u32[]{:S(2)}) collective-permute-start(bf16[2,38,128]{2,0,1:T(2,128)(2,1)} %collective-permute-done.33), channel_id=1, source_target_pairs={{0,16},{16,0},{8,24},{24,8},{32,48},{48,32},{40,56},{56,40},{64,80... | collective-permute-start | bytes 58376 | tf_op jit(solution)/shard_map/ppermute | solution.py:18
  223.1 6.9 %collective-permute-start.35 = (bf16[2,38,128]{2,0,1:T(2,128)(2,1)}, bf16[2,38,128]{2,0,1:T(2,128)(2,1)}, u32[]{:S(2)}, u32[]{:S(2)}) collective-permute-start(bf16[2,38,128]{2,0,1:T(2,128)(2,1)} %collective-permute-done.34), channel_id=1, source_target_pairs={{0,32},{32,0},{8,40},{40,8},{16,48},{48,16},{24,56},{56,24},{64,96... | collective-permute-start | bytes 58376 | tf_op jit(solution)/shard_map/ppermute | solution.py:18
  227.8 14.7 %copy-start.5 = (f32[2,38,8,128]{3,2,1,0:T(8,128)S(1)}, f32[2,38,8,128]{3,2,1,0:T(8,128)}, u32[]{:S(2)}) copy-start(f32[2,38,8,128]{3,2,1,0:T(8,128)} %copy-done.4) | copy-start | bytes 933892
  227.8 14.7 %copy-start.12 = (bf16[4,38,8,1,128]{4,2,1,3,0:T(8,128)(2,1)S(1)}, bf16[4,38,8,1,128]{4,2,1,3,0:T(8,128)(2,1)}, u32[]{:S(2)}) copy-start(bf16[4,38,8,1,128]{4,2,1,3,0:T(8,128)(2,1)} %copy-done.11) | copy-start | bytes 933892
  229.9 10.0 %collective-permute-start.36 = (bf16[2,38,128]{2,0,1:T(2,128)(2,1)}, bf16[2,38,128]{2,0,1:T(2,128)(2,1)S(1)}, u32[]{:S(2)}, u32[]{:S(2)}) collective-permute-start(bf16[2,38,128]{2,0,1:T(2,128)(2,1)} %collective-permute-done.35), channel_id=1, source_target_pairs={{0,64},{64,0},{8,72},{72,8},{16,80},{80,16},{24,88},{88,24},{32,96... | collective-permute-start | bytes 58376 | tf_op jit(solution)/shard_map/ppermute | solution.py:18
  236.4 23.6 %collective-permute-start.32 = (f32[2,38,1,130]{3,2,1,0:T(1,128)}, f32[2,38,1,130]{3,2,1,0:T(1,128)S(1)}, u32[]{:S(2)}, u32[]{:S(2)}) collective-permute-start(f32[2,38,1,130]{3,2,1,0:T(1,128)} %get-tuple-element.108), channel_id=1, source_target_pairs={{1,0},{2,1},{3,2},{4,3},{5,4},{6,5},{7,6},{0,7},{9,8},{10,9},{11,1... | collective-permute-start | bytes 118568 | tf_op jit(solution)/shard_map/ppermute | solution.py:29
  239.9 18.1 %collective-permute-start.37 = (bf16[2,38,128]{2,0,1:T(2,128)(2,1)S(1)}, bf16[2,38,128]{2,0,1:T(2,128)(2,1)}, u32[]{:S(2)}, u32[]{:S(2)}) collective-permute-start(bf16[2,38,128]{2,0,1:T(2,128)(2,1)S(1)} %collective-permute-done.36), channel_id=1, source_target_pairs={{0,128},{128,0},{8,136},{136,8},{16,144},{144,16},{24,152},{152,24... | collective-permute-start | bytes 58376 | tf_op jit(solution)/shard_map/ppermute | solution.py:18
  248.1 19.9 %collective-permute-start.39 = (f32[2,38,1,130]{3,2,1,0:T(1,128)}, f32[2,38,1,130]{3,2,1,0:T(1,128)}, u32[]{:S(2)}, u32[]{:S(2)}) collective-permute-start(f32[2,38,1,130]{3,2,1,0:T(1,128)} %get-tuple-element.109), channel_id=1, source_target_pairs={{0,1},{1,2},{2,3},{3,4},{4,5},{5,6},{6,7},{7,0},{8,9},{9,10},{10,1... | collective-permute-start | bytes 118568 | tf_op jit(solution)/shard_map/ppermute | solution.py:28
  258.0 6.8 %collective-permute-start.38 = (bf16[2,38,128]{2,0,1:T(2,128)(2,1)}, bf16[2,38,128]{2,0,1:T(2,128)(2,1)S(1)}, u32[]{:S(2)}, u32[]{:S(2)}) collective-permute-start(bf16[2,38,128]{2,0,1:T(2,128)(2,1)} %collective-permute-done.37), channel_id=1, source_target_pairs={{0,256},{256,0},{8,264},{264,8},{16,272},{272,16},{24,280},{280,24... | collective-permute-start | bytes 58376 | tf_op jit(solution)/shard_map/ppermute | solution.py:18
  (24 other events, 92.8 us)
